TPU v7x, 32 devices: a whole 2x2x4 slice. The times are simulated.
32 devices in a mesh: dp: 16 (over z, x, core), tensor: 2 (over y).
Axes of the slice: x: 2, y: 2, z: 4, core: 2. Of those that a mesh axis runs over, the one named last changes fastest.
Arguments:
- tokens: bfloat16 [16384, 768], P(('dp', 'tensor')), may hold values from -6 to 6
- lengths: int32 [32], P('dp'), may hold values from 224 to 512, as said below
- cotangent: bfloat16 [16384, 768], P(('dp', 'tensor')), may hold values from -6 to 6
- norm_gain: float32 [2, 2, 768], replicated, may hold values from 0.25 to 1.75
- norm_shift: float32 [2, 2, 768], replicated, may hold values from -1.75 to 1.75
- qkv_weight: bfloat16 [2, 768, 3, 768], P(None, 'dp', None, 'tensor'), may hold values from -0.21875 to 0.21875
- qv_bias: float32 [2, 2, 768], P(None, None, 'tensor'), may hold values from -1.75 to 1.75
- out_weight: bfloat16 [2, 768, 768], P(None, 'tensor', 'dp'), may hold values from -2 to 2
- up_weight: bfloat16 [2, 768, 3072], P(None, 'dp', 'tensor'), may hold values from -0.21875 to 0.21875
- up_bias: float32 [2, 3072], P(None, 'tensor'), may hold values from -1.75 to 1.75
- down_weight: bfloat16 [2, 3072, 768], P(None, 'tensor', 'dp'), may hold values from -0.109375 to 0.109375
- out_bias: float32 [2, 2, 768], replicated, may hold values from -1.75 to 1.75
Outputs:
- final: bfloat16 [16384, 768], P(('dp', 'tensor'))
- token_grad: float32 [16384, 768], P(('dp', 'tensor'))
- grad_norm_gain: float32 [2, 2, 768], replicated
- grad_norm_shift: float32 [2, 2, 768], replicated
- grad_qkv_weight: float32 [2, 768, 3, 768], P(None, 'dp', None, 'tensor')
- grad_qv_bias: float32 [2, 2, 768], P(None, None, 'tensor')
- grad_out_weight: float32 [2, 768, 768], P(None, 'tensor', 'dp')
- grad_up_weight: float32 [2, 768, 3072], P(None, 'dp', 'tensor')
- grad_up_bias: float32 [2, 3072], P(None, 'tensor')
- grad_down_weight: float32 [2, 3072, 768], P(None, 'tensor', 'dp')
- grad_out_bias: float32 [2, 2, 768], replicated
Inputs may be any that keep to these rules, and one draw needn't show every extreme that they name: `lengths`: each clip holds 224 to 512 patches; clip 0 holds exactly 512.
All inputs are finite; a program needn't handle non-finite values.
Results may differ from a plain program's by a relative error of at most 0.015.
Values may be sent and summed in bfloat16 or wider, within the bound.
A program may use at most 192 MiB of HBM per device.

v0:
```python
import functools

import jax
import jax.numpy as jnp
from jax import lax
from jax.experimental import pallas as pl
from jax.experimental.pallas import tpu as pltpu
from jax.sharding import PartitionSpec as P

HEAD_DIM = 64
EPSILON = 1e-06
MESH = pl.DeviceIdType.MESH
VMEM_LIMIT = 60 * 2**20
BF16 = jnp.bfloat16
F32 = jnp.float32
ITEM_COUNT = 8
GATHER_CHAINS = (
    (0, 0, 512, "zxy"),
    (0, 512, 640, "zyx"),
    (1, 0, 256, "yzx"),
    (1, 256, 128, "xzy"),
    (2, 0, 768, "zxy"),
    (2, 768, 768, "zyx"),
    (3, 0, 768, "zxy"),
    (3, 768, 768, "zyx"),
    (4, 0, 512, "xzy"),
    (4, 512, 640, "yzx"),
    (5, 0, 256, "zyx"),
    (5, 256, 128, "zxy"),
    (6, 0, 768, "zxy"),
    (6, 768, 768, "zyx"),
    (7, 0, 768, "xzy"),
    (7, 768, 768, "yzx"),
)
GATHER_TABLE = (
    (12, 32, 8, 36, 20, 0),
    (),
    (-13, 56, -9, 60, -33, -37, -57, -61, -21, 21, 24, -1, 1, 13, -22, 22, -2, 2, -25, 25, 4, -14, 14, 16, -5, 44, -3, 5, 3, -15, 15, -23, -4, 23, -17, 17, 28, -16, -45, 9, -24, -6, -26, 6, 26, -29, 29, 40, -18, 45, -10, 33, -41, 37, -27, 18, 27, -7, 10, 7, -28, -34, 48, -46, -8, -30, 30, 46),
    (-11, 11),
    (-12,),
    (-38, 38, 52),
    (-19, 41, 19, -49, 57, -47, 34, 47, -31, 49),
    (-20, 31, -48, -42),
    (-32, -53, 53, 61),
    (),
    (-39, 42, 39, -35, 35),
    (-40,),
    (-36, -50, 50, -54, 54, -58, 58),
    (-43, 43),
    (-44,),
    (),
    (-62, 62, -51, 51),
    (-55, 55),
    (-52, -56),
    (),
    (-59, 59, -63, 63, -60, -64),
    (),
)


REDUCE_CHAINS = (
    (0, 0, 768, "yzx"),
    (0, 768, 768, "xzy"),
    (1, 0, 768, "yxz"),
    (1, 768, 768, "xyz"),
    (2, 0, 256, "xzy"),
    (2, 256, 128, "yzx"),
    (3, 0, 512, "yxz"),
    (3, 512, 640, "xyz"),
    (4, 0, 768, "yzx"),
    (4, 768, 768, "xzy"),
    (5, 0, 768, "yxz"),
    (5, 768, 768, "xyz"),
    (6, 0, 256, "xyz"),
    (6, 256, 128, "yxz"),
    (7, 0, 512, "yxz"),
    (7, 512, 640, "xyz"),
)
REDUCE_TABLE = (
    (),
    (),
    (),
    (),
    (),
    (4, 0),
    (12, 8),
    (),
    (),
    (-1, 20, 1, -5, 16, 5),
    (),
    (),
    (-9, 24, -13, 9, -21, 13),
    (-2, 21, -17, 2),
    (),
    (-10, 28, -25, -3, 25, -6, 6, 10, -22, 17, -14, -7),
    (-29, 22, 29, -11, 14),
    (32, -26, 36, -23, -18, 26, -30, 18, -15, 30),
    (44, -27),
    (-33, 40, 33, -37, -19, -31, 37),
    (),
    (48, 52),
    (-45,),
    (-34, 34, -41, 45, -49, 41, -53, 49),
    (-35, 53),
    (-46, 56, 46, -42, 60, -50, -54, -38, 38, 54),
    (-47, 50, -55, 42, -57, 57, -39, -51, -61, 61, -58, 58, -43, -62, 62, -59, -63),
)


def places():
    dp = lax.axis_index("dp")
    y = lax.axis_index("tensor")
    return dp // 4, (dp // 2) % 2, dp % 2, y


def partners(z, x, k, y):
    def at(z_, x_, k_, y_):
        return {"dp": (z_ * 2 + x_) * 2 + k_, "tensor": y_}

    along_z = [at((z + step) % 4, x, k, y) for step in (1, 2, 3)]
    return along_z + [at(z, 1 - x, k, y), at(z, x, k, 1 - y), at(z, x, 1 - k, y)]


def greet(peers):
    barrier = pltpu.get_barrier_semaphore()
    for peer in peers:
        pl.semaphore_signal(barrier, inc=1, device_id=peer, device_id_type=MESH)
    pl.semaphore_wait(barrier, len(peers))


def layer_norm(inputs, gain_row, shift_row):
    centered = inputs - jnp.mean(inputs, axis=-1, keepdims=True)
    variance = jnp.mean(centered * centered, axis=-1, keepdims=True)
    return centered * lax.rsqrt(variance + EPSILON) * gain_row + shift_row


def gelu_exact(values):
    return jax.nn.gelu(values, approximate=False)


def mm(left, right, contract):
    return lax.dot_general(left, right, (contract, ((), ())), preferred_element_type=F32)


def halves(array):
    return jnp.stack(jnp.split(array, 2, axis=1))


def heads(array):
    return array.reshape(array.shape[0], -1, HEAD_DIM).transpose(1, 0, 2)


def flat(array):
    return array.transpose(1, 0, 2).reshape(array.shape[1], -1)


class Chains:
    def __init__(self, table, copies, arrived):
        self.table, self.copies, self.arrived = table, copies, arrived
        self.live, self.spot = {}, 0

    def act(self, code):
        if code >= 0:
            key = divmod(code, 4)
            self.live[key] = self.copies(*key)
            for copy in self.live[key]:
                copy.start()
        else:
            key = divmod(-code - 1, 4)
            for copy in self.live.pop(key):
                copy.wait()
            self.arrived(*key)

    def at(self):
        for code in self.table[self.spot]:
            self.act(code)
        self.spot += 1


def axis_index_of(axis, own, order, count):
    return slice(None) if axis in order[:count] else own


def gather_chains(own, held, send, recv, local, peers, place):
    z, x, k, y = place
    mine = {i: pltpu.make_async_copy(own[i], held[i].at[y, z, x, k], local.at[i]) for i in range(len(held))}
    for copy in mine.values():
        copy.start()

    def copies(c, phase):
        i, first, width, order = GATHER_CHAINS[c]
        b, cols = held[i], pl.ds(first, width)

        def remote(source, target, slot, peer):
            return pltpu.make_async_remote_copy(
                source, target, send.at[c, slot], recv.at[c, slot], device_id=peers[peer], device_id_type=MESH
            )

        if phase == 3:
            ref = b.at[:, :, :, k, :, cols]
            return [remote(ref, ref, 5, 5)]
        at = [axis_index_of(axis, own_at, order, phase) for axis, own_at in (("y", y), ("z", z), ("x", x))]
        target = b.at[(*at, k, slice(None), cols)]
        if phase == 0:
            source = own[i].at[:, cols]
        else:
            if i in mine:
                mine.pop(i).wait()
            source = target
        if order[phase] == "z":
            return [remote(source, target, j, j) for j in range(3)]
        return [remote(source, target, 3, 3) if order[phase] == "x" else remote(source, target, 4, 4)]

    return Chains(GATHER_TABLE, copies, lambda c, phase: None)


def matrix(ref, *lead):
    value = ref[lead] if lead else ref[...]
    return value.reshape(-1, value.shape[-1])


def norm_rows(source, gain_row, shift_row, target):
    def block(t, carry):
        rows = pl.ds(pl.multiple_of(t * 128, 128), 128)
        target[rows, :] = layer_norm(source[rows, :], gain_row, shift_row).astype(BF16)
        return carry

    lax.fori_loop(0, source.shape[0] // 128, block, 0)


def turn_rows(source, target, k):
    for c in range(2):
        turned = source[:, c * 384 : (c + 1) * 384].T
        for j in range(8):
            block = c * 8 + j
            target[(block + k) % 2, block // 4, (block // 2) % 2] = turned[j * 48 : (j + 1) * 48]


def forward_kernel(*refs):
    n = ITEM_COUNT
    it = iter(refs)

    def take(count):
        return [next(it) for _ in range(count)]

    own = take(n)
    tokens, lengths, gain, shift, outb, qvb, upb = take(7)
    whole = take(n)
    saved = [take(9) for _ in range(2)]
    (final,) = take(1)
    held = take(n)
    (stream, middle, normed, turned, turned_mid, project, attended, active, slope, probs, qv_all, up_all) = take(12)
    send, recv, local, out_sem, prob_sem, small_send, small_recv, whole_sem = take(8)
    place = z, x, k, y = places()
    peers = partners(z, x, k, y)
    chains = gather_chains(own, held, send, recv, local, peers, place)
    qv_all[y] = qvb[...]
    up_all[y] = upb[...]
    greet(peers)
    chains.at()
    small = [
        pltpu.make_async_remote_copy(
            ref.at[y], ref.at[y], small_send.at[j], small_recv.at[j], device_id=peers[4], device_id_type=MESH
        )
        for j, ref in enumerate((qv_all, up_all))
    ]
    for copy in small:
        copy.start()
    stream[...] = tokens[...].astype(F32)
    length = lengths[y]
    rows = stream.shape[0]
    outgoing = {}

    def save(layer, slot, ref):
        copy = pltpu.make_async_copy(ref, saved[layer][slot], out_sem.at[layer, slot])
        copy.start()
        outgoing[slot] = copy

    def settle(slot):
        if slot in outgoing:
            outgoing.pop(slot).wait()

    back = []

    def keep_weight(i):
        copy = pltpu.make_async_copy(held[i], whole[i], whole_sem.at[i])
        copy.start()
        back.append(copy)

    everything = (slice(None),) * 4
    for layer in range(2):
        w_qkv, w_out, w_up, w_down = held[4 * layer : 4 * layer + 4]
        chains.at()
        settle(2)
        norm_rows(stream, gain[layer, 0:1], shift[layer, 0:1], normed)
        turn_rows(normed, turned, k)
        save(layer, 0, stream)
        save(layer, 2, turned)
        if layer == 0:
            for copy in small:
                copy.wait()
        settle(4)
        for half in range(2):
            chains.at()
            if half == 0:
                keep_weight(4 * layer)

            def third(t, carry):
                cols = pl.ds(pl.multiple_of(t * 384, 128), 384)
                part = mm(normed[...], matrix(w_qkv, half, *everything, cols), ((1,), (0,)))
                bias = jnp.where(t == 1, 0.0, qv_all[half, layer, pl.ds(t // 2, 1)])
                project[half, :, cols] = (part + bias).astype(BF16)
                return carry

            lax.fori_loop(0, 3, third, 0)
        save(layer, 4, project)
        settle(5)

        def pair(j, carry):
            half = j // 3
            at = (j % 3) * 128
            lane = lax.broadcasted_iota(jnp.int32, (1, 128), 1) < 64
            query = project[half, :, pl.ds(pl.multiple_of(at, 128), 128)]
            key = project[half, :, pl.ds(pl.multiple_of(at + 384, 128), 128)]
            value = project[half, :, pl.ds(pl.multiple_of(at + 768, 128), 128)]
            value_t = value.T
            hidden_key = lax.broadcasted_iota(jnp.int32, (rows, 1), 0) >= length
            both = []
            slot = j % 2
            for h in range(2):
                here = lane if h == 0 else jnp.logical_not(lane)
                some = jnp.where(here, key, jnp.zeros_like(key)) * jnp.asarray(HEAD_DIM**-0.5, BF16)
                scores = mm(some, query, ((1,), (1,)))
                scores = jnp.where(hidden_key, -1e30, scores)
                exponent = jnp.exp(scores - jnp.max(scores, axis=0, keepdims=True))
                prob = (exponent * (1.0 / jnp.sum(exponent, axis=0, keepdims=True))).astype(BF16)
                probs[j, h] = prob
                both.append(mm(value_t[h * 64 : (h + 1) * 64], prob, ((1,), (0,))))
            block = jnp.concatenate(both, axis=0).T
            attended[:, pl.ds(pl.multiple_of(j * 128, 128), 128)] = block.astype(BF16)
            return carry

        settle(6)
        for j0 in range(0, 6, 3):
            chains.at()
            lax.fori_loop(j0, j0 + 3, pair, 0)
        save(layer, 5, attended)
        save(layer, 6, probs)
        chains.at()
        keep_weight(4 * layer + 1)
        settle(1)

        def mix(c, carry):
            cols = pl.ds(pl.multiple_of(c * 384, 128), 384)
            total = stream[:, cols] + outb[layer, 0:1, cols]
            for half in range(2):
                total += mm(attended[:, half * 384 : (half + 1) * 384], matrix(w_out, half, pl.ds(2 * c, 2)), ((1,), (1,)))
            middle[:, cols] = total
            return carry

        lax.fori_loop(0, 2, mix, 0)
        save(layer, 1, middle)
        chains.at()
        settle(3)
        norm_rows(middle, gain[layer, 1:2], shift[layer, 1:2], normed)
        turn_rows(normed, turned_mid, k)
        save(layer, 3, turned_mid)
        settle(7)
        settle(8)

        def unit(t, carry):
            half = t // 3
            cols = pl.ds(pl.multiple_of((t % 3) * 512, 128), 512)
            hidden = mm(normed[...], matrix(w_up, half, *everything, cols), ((1,), (0,)))
            hidden = hidden + up_all[half, layer : layer + 1, cols]
            cdf = 0.5 * (1.0 + lax.erf(hidden * (0.5**0.5)))
            density = jnp.exp(-0.5 * hidden * hidden) * 0.3989422804014327
            active[half, :, cols] = (hidden * cdf).astype(BF16)
            slope[half, :, cols] = (cdf + hidden * density).astype(BF16)
            return carry

        for t0 in range(0, 6, 3):
            chains.at()
            if t0 == 0:
                keep_weight(4 * layer + 2)
            lax.fori_loop(t0, t0 + 3, unit, 0)
        save(layer, 7, active)
        save(layer, 8, slope)
        chains.at()
        keep_weight(4 * layer + 3)
        settle(0)

        def close(c, carry):
            cols = pl.ds(pl.multiple_of(c * 384, 128), 384)
            total = middle[:, cols] + outb[layer, 1:2, cols]
            for half in range(2):
                total += mm(active[half], matrix(w_down, half, pl.ds(2 * c, 2)), ((1,), (1,)))
            stream[:, cols] = total
            return carry

        lax.fori_loop(0, 2, close, 0)
    chains.at()
    final[...] = stream[...].astype(BF16)
    for slot in list(outgoing):
        settle(slot)
    for copy in back:
        copy.wait()


def forward(shards, tokens, lengths, gain, shift, outb, qvb, upb):
    rows, width = tokens.shape
    widths = [s.shape[-1] for s in shards]
    full = [(2, 4, 2, 2, 48, w) for w in widths]
    layer_saves = [
        ((rows, width), F32),
        ((rows, width), F32),
        ((2, 4, 2, 48, rows), BF16),
        ((2, 4, 2, 48, rows), BF16),
        ((2, rows, widths[0]), BF16),
        ((rows, width), BF16),
        ((6, 2, rows, rows), BF16),
        ((2, rows, widths[2]), BF16),
        ((2, rows, widths[2]), BF16),
    ]
    any_spec = pl.BlockSpec(memory_space=pl.ANY)
    vmem_spec = pl.BlockSpec(memory_space=pltpu.VMEM)
    out_shape = (
        [jax.ShapeDtypeStruct(f, BF16) for f in full]
        + [jax.ShapeDtypeStruct(s, t) for s, t in layer_saves * 2]
        + [jax.ShapeDtypeStruct((rows, width), BF16)]
    )
    by_slot = {j: pltpu.VMEM(*layer_saves[j]) for j in range(9)}
    outs = pl.pallas_call(
        forward_kernel,
        out_shape=out_shape,
        in_specs=[any_spec] * ITEM_COUNT + [vmem_spec, pl.BlockSpec(memory_space=pltpu.SMEM)] + [vmem_spec] * 5,
        out_specs=[any_spec] * (ITEM_COUNT + 18) + [vmem_spec],
        scratch_shapes=[pltpu.VMEM(f, BF16) for f in full]
        + [
            by_slot[0],
            by_slot[1],
            pltpu.VMEM((rows, width), BF16),
            by_slot[2],
            by_slot[3],
            by_slot[4],
            by_slot[5],
            by_slot[7],
            by_slot[8],
            by_slot[6],
            pltpu.VMEM((2, *qvb.shape), F32),
            pltpu.VMEM((2, *upb.shape), F32),
            pltpu.SemaphoreType.DMA((len(GATHER_CHAINS), 6)),
            pltpu.SemaphoreType.DMA((len(GATHER_CHAINS), 6)),
            pltpu.SemaphoreType.DMA((ITEM_COUNT,)),
            pltpu.SemaphoreType.DMA((2, 9)),
            pltpu.SemaphoreType.DMA((2,)),
            pltpu.SemaphoreType.DMA((2,)),
            pltpu.SemaphoreType.DMA((2,)),
            pltpu.SemaphoreType.DMA((ITEM_COUNT,)),
        ],
        compiler_params=pltpu.CompilerParams(
            collective_id=0, has_side_effects=True, vmem_limit_bytes=VMEM_LIMIT
        ),
        name="forward",
    )(*shards, tokens, lengths, gain, shift, outb, qvb, upb)
    return outs[:ITEM_COUNT], [outs[ITEM_COUNT + 9 * l : ITEM_COUNT + 9 * l + 9] for l in range(2)], outs[-1]


def norm_back(source, upstream, gain_row, gradient, rounded):
    def block(t, sums):
        rows = pl.ds(pl.multiple_of(t * 64, 64), 64)
        inputs = source[rows, :]
        centered = inputs - jnp.mean(inputs, axis=-1, keepdims=True)
        rate = lax.rsqrt(jnp.mean(centered * centered, axis=-1, keepdims=True) + EPSILON)
        unit = centered * rate
        above = upstream[rows, :]
        pull = above * gain_row
        along = jnp.mean(pull * unit, axis=-1, keepdims=True)
        total = gradient[rows, :] + rate * (pull - jnp.mean(pull, axis=-1, keepdims=True) - unit * along)
        gradient[rows, :] = total
        if rounded is not None:
            rounded[rows, :] = total.astype(BF16)
        return (
            sums[0] + jnp.sum(above * unit, axis=0, keepdims=True),
            sums[1] + jnp.sum(above, axis=0, keepdims=True),
            sums[2] + jnp.sum(total, axis=0, keepdims=True),
        )

    zero = jnp.zeros((1, source.shape[1]), F32)
    return lax.fori_loop(0, source.shape[0] // 64, block, (zero, zero, zero))


def backward_kernel(*refs):
    n = ITEM_COUNT
    it = iter(refs)

    def take(count):
        return [next(it) for _ in range(count)]

    whole = take(n)
    saved = [take(9) for _ in range(2)]
    cotangent, lengths, gain = take(3)
    out_q, out_o, out_u, out_d, token_grad, sums = take(6)
    outs = (out_q, out_o, out_u, out_d)
    (slot_a, slot_b, stream, middle, turned, turned_mid, project, attended, active, slope, probs) = take(11)
    (gradient, upstream, rounded, left, dattended, dproject) = take(6)
    held = take(4)
    (to_core, from_core) = take(2)
    arrivals = [take(3) for _ in REDUCE_CHAINS]
    small_c, small_x, small_y, small_z = take(4)
    (fetch_sem, prob_sem, core_send, core_recv, send, recv, credit, small_send, small_recv, last_sem) = take(10)
    place = z, x, k, y = places()
    peers = partners(z, x, k, y)
    rows = stream.shape[0]

    fetches = {}

    def fetch(name, pairs):
        fetches[name] = [pltpu.make_async_copy(s, t, fetch_sem.at[name, j]) for j, (s, t) in enumerate(pairs)]
        for copy in fetches[name]:
            copy.start()

    def ready(name):
        for copy in fetches.pop(name):
            copy.wait()

    def weights_into(slot, layer, kind):
        w_qkv, w_out, w_up, w_down = whole[4 * layer : 4 * layer + 4]
        if kind == "d":
            return [(w_down, slot)]
        if kind == "u":
            return [(w_up, slot)]
        lead = (slice(None),) * 5
        return [(w_qkv, slot.at[(*lead, pl.ds(0, 1152))]), (w_out, slot.at[(*lead, pl.ds(1152, 384))])]

    SLOT_A, SLOT_B, STREAM, MIDDLE, TURNED, TURNED_MID, PROJECT, ATTENDED, ACTIVE, SLOPE, COT = range(11)
    buffers = {
        STREAM: (stream, 0),
        MIDDLE: (middle, 1),
        TURNED: (turned, 2),
        TURNED_MID: (turned_mid, 3),
        PROJECT: (project, 4),
        ATTENDED: (attended, 5),
        ACTIVE: (active, 7),
        SLOPE: (slope, 8),
    }

    def fetch_saved(name, layer):
        target, index = buffers[name]
        fetch(name, [(saved[layer][index], target)])

    def prob_copy(layer, j):
        return pltpu.make_async_copy(saved[layer][6].at[j], probs.at[j % 2], prob_sem.at[j % 2])

    fetch(COT, [(cotangent, rounded)])
    fetch(SLOT_A, weights_into(slot_a, 1, "d"))
    for name in (SLOPE, ACTIVE):
        fetch_saved(name, 1)
    fetch(SLOT_B, weights_into(slot_b, 1, "u"))
    for name in (TURNED_MID, MIDDLE, ATTENDED, PROJECT, TURNED, STREAM):
        fetch_saved(name, 1)
    prob_copy(1, 0).start()
    slots = {("d", 1): (SLOT_A, slot_a), ("u", 1): (SLOT_B, slot_b), ("q", 1): (SLOT_A, slot_a),
             ("d", 0): (SLOT_B, slot_b), ("u", 0): (SLOT_A, slot_a), ("q", 0): (SLOT_B, slot_b)}
    greet(peers)

    kinds = [(1, 3), (1, 2), (1, 1), (1, 0), (0, 3), (0, 2), (0, 1), (0, 0)]

    def core_copy(r, half):
        width = held[kinds[r][1]].shape[-1]
        at = (half, slice(None), slice(None), slice(None), pl.ds(0, width))
        return pltpu.make_async_remote_copy(
            to_core.at[at], from_core.at[at], core_send.at[r, half], core_recv.at[r, half],
            device_id=peers[5], device_id_type=MESH,
        )

    def take_core(r):
        b = held[kinds[r][1]]
        width = b.shape[-1]
        for half in range(2):
            core_copy(r, half).wait()

        def block(t, carry):
            at = (t // 8, (t // 2) % 4, t % 2)
            b[at] = b[at] + from_core[(*at, slice(None), pl.ds(0, width))]
            return carry

        lax.fori_loop(0, 16, block, 0)
        if r < n - 1:
            for half in range(2):
                pl.semaphore_signal(credit.at[half], inc=1, device_id=peers[5], device_id_type=MESH)

    def rest_of(order, phase):
        return [(axis, size) for axis, size in (("y", 2), ("z", 4), ("x", 2)) if axis in order[phase + 1 :]]

    def copies(c, phase):
        r, first, width, order = REDUCE_CHAINS[c]
        b, cols = held[kinds[r][1]], pl.ds(first, width)
        target = arrivals[c][phase]
        left_over = order[phase + 1 :]

        def block(axis, there):
            at = []
            for name, own_at in (("y", y), ("z", z), ("x", x)):
                at.append(there if name == axis else slice(None) if name in left_over else own_at)
            return b.at[(*at, slice(None), cols)]

        def remote(source, there, slot, peer):
            return pltpu.make_async_remote_copy(
                source, there, send.at[c, slot], recv.at[c, slot], device_id=peers[peer], device_id_type=MESH
            )

        if order[phase] == "z":
            return [remote(block("z", (z + 1 + j) % 4), target.at[j], j, j) for j in range(3)]
        if order[phase] == "x":
            return [remote(block("x", 1 - x), target, 3, 3)]
        return [remote(block("y", 1 - y), target, 4, 4)]

    def arrived(c, phase):
        r, first, width, order = REDUCE_CHAINS[c]
        layer, kind = kinds[r]
        b, cols = held[kind], pl.ds(first, width)
        source = arrivals[c][phase]
        rest = rest_of(order, phase)
        count = 1
        for _, size in rest:
            count *= size

        def total(t):
            at, inner, stride = {}, [], 1
            for axis, size in reversed(rest):
                at[axis] = (t // stride) % size
                stride *= size
            inner = [at[axis] for axis, _ in rest]
            spot = (at.get("y", y), at.get("z", z), at.get("x", x), slice(None), cols)
            value = b[spot].astype(F32)
            if order[phase] == "z":
                for j in range(3):
                    value += source[(j, *inner)].astype(F32)
            else:
                value += source[tuple(inner)].astype(F32) if inner else source[...].astype(F32)
            return spot, value

        if not rest:
            outs[kind][layer, :, cols] = total(0)[1]
        else:

            def block(t, carry):
                spot, value = total(t)
                b[spot] = value.astype(BF16)
                return carry

            lax.fori_loop(0, count, block, 0)

    chains = Chains(REDUCE_TABLE, copies, arrived)

    def weight_gradient(r, lhs, rhs):
        b = held[kinds[r][1]]
        width = b.shape[-1]
        size = 512 if width % 512 == 0 else 384

        def one(half, carry):
            def chunk(t, inner):
                cols = pl.ds(pl.multiple_of(t * size, 128), size)
                value = mm(lhs[...].reshape(768, rows), rhs(half, cols), ((1,), (0,))).astype(BF16)
                b[half, :, :, :, cols] = value[:384].reshape(4, 2, 48, size)
                to_core[half, :, :, :, cols] = value[384:].reshape(4, 2, 48, size)
                return inner

            lax.fori_loop(0, width // size, chunk, 0)
            if r > 0:
                pl.semaphore_wait(credit.at[half], 1)
            core_copy(r, half).start()
            return carry

        lax.fori_loop(0, 2, one, 0)

    chains.at()
    chains.at()
    ready(COT)
    keep = lax.broadcasted_iota(jnp.int32, (rows, 1), 0) < lengths[y]
    gradient[...] = jnp.where(keep, rounded[...].astype(F32), 0.0)
    rounded[...] = gradient[...].astype(BF16)
    everything = (slice(None),) * 4

    def place_at(*taken):
        for r in taken:
            take_core(r)
        chains.at()

    for layer in (1, 0):
        first = 0 if layer == 1 else 4
        place_at()
        sums[layer, 2:3, 768:1536] = jnp.sum(gradient[...], axis=0, keepdims=True)
        turn_rows(rounded, left, k)
        name, w_down = slots["d", layer]
        ready(ACTIVE)
        place_at()
        weight_gradient(first, left, lambda half, cols: active[half, :, cols])
        ready(name)
        ready(SLOPE)
        place_at()

        def unit(t, carry):
            half = t // 3
            cols = pl.ds(pl.multiple_of((t % 3) * 512, 128), 512)
            dact = mm(rounded[...], matrix(w_down, half, *everything, cols), ((1,), (0,)))
            dhidden = (dact * slope[half, :, cols].astype(F32)).astype(BF16)
            slope[half, :, cols] = dhidden
            sums[layer, pl.ds(4 + half, 1), cols] = jnp.sum(dhidden.astype(F32), axis=0, keepdims=True)
            return carry

        lax.fori_loop(0, 6, unit, 0)
        if layer == 1:
            fetch(SLOT_A, weights_into(slot_a, 1, "q"))
            fetch_saved(ACTIVE, 0)
        else:
            fetch(SLOT_B, weights_into(slot_b, 0, "q"))
        name, w_up = slots["u", layer]
        ready(name)
        ready(TURNED_MID)
        place_at(first)
        weight_gradient(first + 1, turned_mid, lambda half, cols: slope[half, :, cols])
        place_at(first + 1)

        def pull_up(c, carry):
            total = mm(slope[0], matrix(w_up, 0, pl.ds(2 * c, 2)), ((1,), (1,)))
            total += mm(slope[1], matrix(w_up, 1, pl.ds(2 * c, 2)), ((1,), (1,)))
            upstream[:, pl.ds(pl.multiple_of(c * 384, 128), 384)] = total
            return carry

        lax.fori_loop(0, 2, pull_up, 0)
        if layer == 1:
            fetch(SLOT_B, weights_into(slot_b, 0, "d"))
            fetch_saved(SLOPE, 0)
            fetch_saved(TURNED_MID, 0)
        ready(MIDDLE)
        place_at()
        gain_sum, shift_sum, bias_sum = norm_back(middle, upstream, gain[layer, 1:2], gradient, rounded)
        sums[layer, 0:1, 768:1536] = gain_sum
        sums[layer, 1:2, 768:1536] = shift_sum
        sums[layer, 2:3, 0:768] = bias_sum
        if layer == 1:
            fetch_saved(MIDDLE, 0)
        name, w_qo = slots["q", layer]
        ready(name)
        ready(ATTENDED)
        place_at()
        turn_rows(rounded, left, k)
        weight_gradient(first + 2, left, lambda half, cols: attended[:, pl.ds(pl.multiple_of(half * 384, 128), 384)])

        def pull_out(half, carry):
            dattended[half] = mm(rounded[...], matrix(w_qo, half, *everything, pl.ds(1152, 384)), ((1,), (0,))).astype(BF16)
            return carry

        lax.fori_loop(0, 2, pull_out, 0)
        if layer == 1:
            fetch_saved(ATTENDED, 0)
        ready(PROJECT)
        scale = HEAD_DIM**-0.5

        def pair(j, carry):
            half = j // 3
            at = (j % 3) * 128
            prob_copy(layer, j).wait()

            @pl.when(j < 5)
            def _():
                prob_copy(layer, j + 1).start()

            lane = lax.broadcasted_iota(jnp.int32, (1, 128), 1) < 64
            columns = [pl.ds(pl.multiple_of(at + t * 384, 128), 128) for t in range(3)]
            query, key, value = (project[half, :, c] for c in columns)
            above = dattended[half, :, columns[0]]
            key_t = key.T
            dkeys, dvalues, dqueries = [], [], []
            for h in range(2):
                here = lane if h == 0 else jnp.logical_not(lane)
                prob = probs[j % 2, h]
                dprob = mm(jnp.where(here, value, jnp.zeros_like(value)), above, ((1,), (1,)))
                prob32 = prob.astype(F32)
                both = prob32 * dprob
                dscore = (both - prob32 * jnp.sum(both, axis=0, keepdims=True)).astype(BF16)
                dvalues.append(mm(prob, above, ((1,), (0,))))
                dkeys.append(mm(dscore, query, ((1,), (0,))))
                dqueries.append(mm(key_t[h * 64 : (h + 1) * 64], dscore, ((1,), (0,))))
            dproject[half, :, columns[0]] = (jnp.concatenate(dqueries, axis=0) * scale).T.astype(BF16)
            dproject[half, :, columns[1]] = (jnp.where(lane, dkeys[0], dkeys[1]) * scale).astype(BF16)
            dproject[half, :, columns[2]] = jnp.where(lane, dvalues[0], dvalues[1]).astype(BF16)
            return carry

        place_at(first + 2)
        lax.fori_loop(0, 3, pair, 0)
        place_at()
        lax.fori_loop(3, 6, pair, 0)
        if layer == 1:
            fetch_saved(PROJECT, 0)
            prob_copy(0, 0).start()
        ready(TURNED)
        place_at()
        for half in range(2):
            for t in (0, 2):
                sums[layer, 3:4, (t // 2) * 768 + half * 384 : (t // 2) * 768 + half * 384 + 384] = jnp.sum(
                    dproject[half, :, t * 384 : (t + 1) * 384].astype(F32), axis=0, keepdims=True
                )
        weight_gradient(first + 3, turned, lambda half, cols: dproject[half, :, cols])
        place_at(first + 3)

        def pull_qkv(c, carry):
            rest = (slice(None),) * 3
            total = mm(dproject[0], matrix(w_qo, 0, pl.ds(2 * c, 2), *rest, pl.ds(0, 1152)), ((1,), (1,)))
            total += mm(dproject[1], matrix(w_qo, 1, pl.ds(2 * c, 2), *rest, pl.ds(0, 1152)), ((1,), (1,)))
            upstream[:, pl.ds(pl.multiple_of(c * 384, 128), 384)] = total
            return carry

        lax.fori_loop(0, 2, pull_qkv, 0)
        if layer == 1:
            fetch(SLOT_A, weights_into(slot_a, 0, "u"))
            fetch_saved(TURNED, 0)
        ready(STREAM)
        place_at()
        gain_sum, shift_sum, _ = norm_back(stream, upstream, gain[layer, 0:1], gradient, rounded if layer == 1 else None)
        sums[layer, 0:1, 0:768] = gain_sum
        sums[layer, 1:2, 0:768] = shift_sum
        if layer == 1:
            fetch_saved(STREAM, 0)
    last = pltpu.make_async_copy(gradient, token_grad, last_sem)
    last.start()

    sums[:, 6:8, :] = jnp.zeros((2, 2, 1536), F32)

    def exchange(slot, target, peer):
        copy = pltpu.make_async_remote_copy(
            sums, target, small_send.at[slot], small_recv.at[slot], device_id=peers[peer], device_id_type=MESH
        )
        copy.start()
        return copy

    tail = chains.table[chains.spot]
    parts = [tail[len(tail) * j // 4 : len(tail) * (j + 1) // 4] for j in range(4)]
    for slot, (target, peer) in enumerate(((small_c, 5), (small_x, 3), (small_y, 4))):
        copy = exchange(slot, target, peer)
        for code in parts[slot]:
            chains.act(code)
        copy.wait()
        sums[...] += target[...]
    small_z[z] = sums[...]
    across = [exchange(3 + j, small_z.at[z], j) for j in range(3)]
    for code in parts[3]:
        chains.act(code)
    for copy in across:
        copy.wait()
    sums[...] = (small_z[0] + small_z[1]) + (small_z[2] + small_z[3])
    last.wait()


def backward(whole, saved, cotangent, lengths, gain):
    rows, width = cotangent.shape
    widths = [w.shape[-1] for w in whole[:4]]
    any_spec = pl.BlockSpec(memory_space=pl.ANY)
    vmem_spec = pl.BlockSpec(memory_space=pltpu.VMEM)

    def blocks(*lead):
        return [pltpu.VMEM((*lead, 48, w), BF16) for w in widths]

    def arrival_shapes():
        sizes, shapes = {"y": 2, "z": 4, "x": 2}, []
        for _, _, columns, order in REDUCE_CHAINS:
            for phase in range(3):
                lead = [3] if order[phase] == "z" else []
                lead += [sizes[axis] for axis in "yzx" if axis in order[phase + 1 :]]
                shapes.append(pltpu.VMEM((*lead, 48, columns), BF16))
        return shapes

    wide = widths[2]
    small = (2, 8, wide)
    outs = pl.pallas_call(
        backward_kernel,
        out_shape=[jax.ShapeDtypeStruct((2, 48, w), F32) for w in widths]
        + [jax.ShapeDtypeStruct((rows, width), F32), jax.ShapeDtypeStruct(small, F32)],
        in_specs=[any_spec] * (ITEM_COUNT + 18 + 1) + [pl.BlockSpec(memory_space=pltpu.SMEM), vmem_spec],
        out_specs=[vmem_spec] * 4 + [any_spec, vmem_spec],
        scratch_shapes=[
            pltpu.VMEM((2, 4, 2, 2, 48, wide), BF16),
            pltpu.VMEM((2, 4, 2, 2, 48, wide), BF16),
            pltpu.VMEM((rows, width), F32),
            pltpu.VMEM((rows, width), F32),
            pltpu.VMEM((2, 4, 2, 48, rows), BF16),
            pltpu.VMEM((2, 4, 2, 48, rows), BF16),
            pltpu.VMEM((2, rows, widths[0]), BF16),
            pltpu.VMEM((rows, width), BF16),
            pltpu.VMEM((2, rows, wide), BF16),
            pltpu.VMEM((2, rows, wide), BF16),
            pltpu.VMEM((2, 2, rows, rows), BF16),
            pltpu.VMEM((rows, width), F32),
            pltpu.VMEM((rows, width), F32),
            pltpu.VMEM((rows, width), BF16),
            pltpu.VMEM((2, 4, 2, 48, rows), BF16),
            pltpu.VMEM((2, rows, width // 2), BF16),
            pltpu.VMEM((2, rows, widths[0]), BF16),
        ]
        + blocks(2, 4, 2)
        + [pltpu.VMEM((2, 4, 2, 48, wide), BF16), pltpu.VMEM((2, 4, 2, 48, wide), BF16)]
        + arrival_shapes()
        + [pltpu.VMEM(small, F32)] * 3
        + [pltpu.VMEM((4, *small), F32)]
        + [
            pltpu.SemaphoreType.DMA((11, 2)),
            pltpu.SemaphoreType.DMA((2,)),
            pltpu.SemaphoreType.DMA((ITEM_COUNT, 2)),
            pltpu.SemaphoreType.DMA((ITEM_COUNT, 2)),
            pltpu.SemaphoreType.DMA((len(REDUCE_CHAINS), 5)),
            pltpu.SemaphoreType.DMA((len(REDUCE_CHAINS), 5)),
            pltpu.SemaphoreType.REGULAR((2,)),
            pltpu.SemaphoreType.DMA((6,)),
            pltpu.SemaphoreType.DMA((6,)),
            pltpu.SemaphoreType.DMA,
        ],
        compiler_params=pltpu.CompilerParams(
            collective_id=1, has_side_effects=True, vmem_limit_bytes=63 * 2**20
        ),
        name="backward",
    )(*whole, *saved[0], *saved[1], cotangent, lengths, gain)
    return outs


def generic_body(dp_size, tokens, lengths, cotangent, norm_gain, norm_shift, qkv_weight, qv_bias,
         out_weight, up_weight, up_bias, down_weight, out_bias):
    part = lax.axis_index("tensor")
    layers = norm_gain.shape[0]
    rows, width = tokens.shape
    length = lax.dynamic_index_in_dim(lengths, part, keepdims=False)
    keep = jnp.arange(rows, dtype=jnp.int32) < length
    own = qkv_weight.shape[1]
    shards = []
    for layer in range(layers):
        shards += [
            qkv_weight[layer].reshape(own, -1),
            out_weight[layer].T,
            up_weight[layer],
            down_weight[layer].T,
        ]
    if False:
        full = [w.reshape(2, width, -1) for w in gather_weights(shards)]
    else:
        full = [
            lax.all_gather(s, ("tensor", "dp"), axis=0).reshape(2, width, -1) for s in shards
        ]
    qv_all = lax.all_gather(qv_bias, "tensor", axis=0)
    upb_all = lax.all_gather(up_bias, "tensor", axis=0)
    scale = HEAD_DIM**-0.5
    stream = tokens.astype(F32)
    saved = []
    for layer in range(layers):
        w_qkv, w_out, w_up, w_down = full[4 * layer : 4 * layer + 4]
        normed = layer_norm(stream, norm_gain[layer, 0], norm_shift[layer, 0]).astype(BF16)
        project = []
        for t in range(2):
            b = jnp.concatenate([qv_all[t, layer, 0], jnp.zeros_like(qv_all[t, layer, 0]), qv_all[t, layer, 1]])
            project.append((mm(normed, w_qkv[t], ((1,), (0,))) + b).astype(BF16))
        third = width // 2
        q, key, val = (
            heads(jnp.concatenate([project[t][:, j * third : (j + 1) * third] for t in range(2)], axis=1))
            for j in range(3)
        )
        scores = jnp.einsum("hqd,hkd->hqk", q, key, preferred_element_type=F32) * scale
        scores = jnp.where(keep[None, None, :], scores, -1e30)
        highest = jnp.max(scores, axis=-1, keepdims=True)
        exponent = jnp.exp(scores - highest)
        probs32 = exponent / jnp.sum(exponent, axis=-1, keepdims=True)
        probs = probs32.astype(BF16)
        attended = flat(jnp.einsum("hqk,hkd->hqd", probs, val, preferred_element_type=F32)).astype(BF16)
        branch = sum(mm(attended[:, t * third : (t + 1) * third], w_out[t], ((1,), (1,))) for t in range(2))
        middle = stream + branch + out_bias[layer, 0]
        normed_mid = layer_norm(middle, norm_gain[layer, 1], norm_shift[layer, 1]).astype(BF16)
        hidden = [mm(normed_mid, w_up[t], ((1,), (0,))) + upb_all[t, layer] for t in range(2)]
        activated = [gelu_exact(h).astype(BF16) for h in hidden]
        branch_mlp = sum(mm(activated[t], w_down[t], ((1,), (1,))) for t in range(2))
        saved.append((stream, middle, normed, q, key, val, probs, attended, normed_mid, hidden, activated))
        stream = middle + branch_mlp + out_bias[layer, 1]
    final = stream.astype(BF16)
    gradient = cotangent.astype(F32) * keep.astype(F32)[:, None]
    grads = [None] * (4 * layers)
    gain, shift, outb, qvb, upb = ([None] * layers for _ in range(5))
    for layer in reversed(range(layers)):
        stream_in, middle, normed, q, key, val, probs, attended, normed_mid, hidden, activated = saved[layer]
        w_qkv, w_out, w_up, w_down = full[4 * layer : 4 * layer + 4]
        third = width // 2
        bias_late = jnp.sum(gradient, axis=0)
        dout = gradient.astype(BF16)
        grads[4 * layer + 3] = jnp.stack([mm(dout, activated[t], ((0,), (0,))).astype(BF16) for t in range(2)])
        dhidden = []
        for t in range(2):
            dact = mm(dout, w_down[t], ((1,), (0,)))
            dhidden.append(jax.vjp(gelu_exact, hidden[t])[1](dact)[0].astype(BF16))
        upb[layer] = jnp.stack([jnp.sum(d.astype(F32), axis=0) for d in dhidden])
        grads[4 * layer + 2] = jnp.stack([mm(normed_mid, d, ((0,), (0,))).astype(BF16) for d in dhidden])
        dnormed_mid = sum(mm(dhidden[t], w_up[t], ((1,), (1,))) for t in range(2))
        pull = jax.vjp(layer_norm, middle, norm_gain[layer, 1], norm_shift[layer, 1])[1]
        dmid, gain_late, shift_late = pull(dnormed_mid)
        dmiddle = gradient + dmid
        bias_early = jnp.sum(dmiddle, axis=0)
        dbranch = dmiddle.astype(BF16)
        dout_t = mm(dbranch, attended, ((0,), (0,))).astype(BF16)
        grads[4 * layer + 1] = halves(dout_t)
        dattended = heads(jnp.concatenate([mm(dbranch, w_out[t], ((1,), (0,))) for t in range(2)], axis=1).astype(BF16))
        p = probs.astype(F32)
        dval = jnp.einsum("hqk,hqd->hkd", probs, dattended, preferred_element_type=F32)
        dprobs = jnp.einsum("hqd,hkd->hqk", dattended, val, preferred_element_type=F32)
        dscores = (p * (dprobs - jnp.sum(p * dprobs, axis=-1, keepdims=True))).astype(BF16)
        dquery = jnp.einsum("hqk,hkd->hqd", dscores, key, preferred_element_type=F32) * scale
        dkey = jnp.einsum("hqk,hqd->hkd", dscores, q, preferred_element_type=F32) * scale
        parts = [flat(a).astype(BF16) for a in (dquery, dkey, dval)]
        dproject = [
            jnp.concatenate([a[:, t * third : (t + 1) * third] for a in parts], axis=1) for t in range(2)
        ]
        qvb[layer] = jnp.stack([jnp.sum(parts[0].astype(F32), axis=0), jnp.sum(parts[2].astype(F32), axis=0)])
        grads[4 * layer] = jnp.stack([mm(normed, d, ((0,), (0,))).astype(BF16) for d in dproject])
        dnormed = sum(mm(dproject[t], w_qkv[t], ((1,), (1,))) for t in range(2))
        pull = jax.vjp(layer_norm, stream_in, norm_gain[layer, 0], norm_shift[layer, 0])[1]
        dfirst, gain_early, shift_early = pull(dnormed)
        gradient = dmiddle + dfirst
        gain[layer] = jnp.stack([gain_early, gain_late])
        shift[layer] = jnp.stack([shift_early, shift_late])
        outb[layer] = jnp.stack([bias_early, bias_late])
    if False:
        reduced = reduce_gradients([g.reshape(2, 4, 2, 2, 48, -1) for g in grads])
    else:
        reduced = [
            lax.psum_scatter(
                g.reshape(2 * dp_size, own, -1).astype(F32), ("tensor", "dp"), scatter_dimension=0
            )
            for g in grads
        ]
    g_gain, g_shift, g_outb, g_qvb, g_upb = lax.psum(
        (jnp.stack(gain), jnp.stack(shift), jnp.stack(outb), jnp.stack(qvb), jnp.stack(upb)),
        ("dp", "tensor"),
    )
    g_qvb = lax.dynamic_slice_in_dim(g_qvb, part * qv_bias.shape[2], qv_bias.shape[2], axis=2)
    g_upb = lax.dynamic_index_in_dim(g_upb, part, axis=1, keepdims=False)
    g_qkv = jnp.stack([reduced[4 * l].reshape(own, 3, -1) for l in range(layers)])
    g_out = jnp.stack([reduced[4 * l + 1].T for l in range(layers)])
    g_up = jnp.stack([reduced[4 * l + 2] for l in range(layers)])
    g_down = jnp.stack([reduced[4 * l + 3].T for l in range(layers)])
    return (final, gradient, g_gain, g_shift, g_qkv, g_qvb, g_out, g_up, g_upb, g_down, g_outb)


def fused_body(tokens, lengths, cotangent, norm_gain, norm_shift, qkv_weight, qv_bias, out_weight, up_weight,
               up_bias, down_weight, out_bias):
    part = lax.axis_index("tensor")
    layers = norm_gain.shape[0]
    rows, width = tokens.shape
    third = width // 2
    own = qkv_weight.shape[1]
    shards = []
    for layer in range(layers):
        shards += [
            qkv_weight[layer].reshape(own, -1),
            out_weight[layer].T,
            up_weight[layer],
            down_weight[layer].T,
        ]
    full, saved, final = forward(shards, tokens, lengths, norm_gain, norm_shift, out_bias, qv_bias, up_bias)
    g_qkv, g_out, g_up, g_down, token_grad, small = backward(full, saved, cotangent, lengths, norm_gain)
    g_gain, g_shift, g_outb, g_qvb = (small[:, j].reshape(layers, 2, width) for j in range(4))
    g_upb = lax.dynamic_index_in_dim(small, 4 + part, axis=1, keepdims=False)
    g_qvb = lax.dynamic_slice_in_dim(g_qvb, part * third, third, axis=2)
    return (
        final,
        token_grad,
        g_gain,
        g_shift,
        g_qkv.reshape(layers, own, 3, third),
        g_qvb,
        g_out.transpose(0, 2, 1),
        g_up,
        g_upb,
        g_down.transpose(0, 2, 1),
        g_outb,
    )


def solution(mesh):
    use_kernels = mesh.shape["dp"] == 16 and mesh.shape["tensor"] == 2
    return jax.shard_map(
        fused_body if use_kernels else functools.partial(generic_body, mesh.shape["dp"]),
        mesh=mesh,
        in_specs=(
            P(("dp", "tensor"), None),
            P("dp"),
            P(("dp", "tensor"), None),
            P(),
            P(),
            P(None, "dp", None, "tensor"),
            P(None, None, "tensor"),
            P(None, "tensor", "dp"),
            P(None, "dp", "tensor"),
            P(None, "tensor"),
            P(None, "tensor", "dp"),
            P(),
        ),
        out_specs=(
            P(("dp", "tensor"), None),
            P(("dp", "tensor"), None),
            P(),
            P(),
            P(None, "dp", None, "tensor"),
            P(None, None, "tensor"),
            P(None, "tensor", "dp"),
            P(None, "dp", "tensor"),
            P(None, "tensor"),
            P(None, "tensor", "dp"),
            P(),
        ),
        check_vma=False,
    )
```

profile of v0, /device:TPU:0, one launch (start us, length us, event | category | flops | bytes accessed | tf_op | source)
XLA Modules:
  0.0 318.1 jit_solution(13490067770446215761)
XLA Ops:
  0.6 1.0 fusion
  1.6 0.1 copy.26
  1.7 0.7 copy.31
  2.3 1.4 slice_bitcast_fusion.4
  3.8 1.7 slice_bitcast_fusion.1
  5.5 1.7 slice_bitcast_fusion
  7.2 0.1 copy.27
  7.2 0.7 copy.32
  7.9 139.2 %forward.1 = (bf16[2,4,2,2,48,1152]{5,4,3,2,1,0:T(8,128)(2,1)}, bf16[2,4,2,2,48,384]{5,4,3,2,1,0:T(8,128)(2,1)}, bf16[2,4,2,2,48,1536]{5,4,3,2,1,0:T(8,128)(2,1)...) custom-call(bf16[48,1152]{1,0:T(8,128)(2,1)} %bitcast.38, ...), custom_call_target="tpu_custom_call" | custom-call | tf_op jit(solution)/shard_map/forward/pallas_call | solution.py:433
  147.1 160.4 %backward.1 = (f32[2,48,1152]{2,1,0:T(8,128)}, f32[2,48,384]{2,1,0:T(8,128)}, f32[2,48,1536]{2,1,0:T(8,128)}, f32[2,48,1536]{2,1,0:T(8,128)}, f32[512,768]{1,0:T(8,128)}, /*index=5*/f32[2,8,1536]{2,1,0:T(8,128)}) custom-call(bf16[2,4,2,2,48,1152]{5,4,3,2,1,0:T(8,128)(2,1)} %get-tuple-element.45.refs_0_, ...), custom_call_target="tpu_custom_call" | custom-call | tf_op jit(solution)/shard_map/backward/pallas_call | solution.py:877
  307.5 1.4 slice_reduce_fusion
  308.9 0.6 reshape_squeeze.20
  309.5 0.6 reshape_squeeze.21
  310.1 1.8 copy.35
  312.0 0.6 constant_dynamic-slice_fusion.1
  312.6 0.6 copy.36
  313.2 0.6 reshape_squeeze.23
  313.8 0.9 copy.42
  314.7 0.0 copy-done
  314.7 1.1 copy.43
  315.8 0.7 copy.44
  316.5 0.0 copy-done.3
  316.5 0.8 copy.45
  317.3 0.8 copy.46
  (9 shorter events, 0.0 us)
Async XLA Ops:
  147.1 166.7 %copy-start.1 = (bf16[512,768]{1,0:T(8,128)(2,1)S(1)}, bf16[512,768]{1,0:T(8,128)(2,1)}, u32[]{:S(2)}) copy-start(bf16[512,768]{1,0:T(8,128)(2,1)} %get-tuple-element.123) | copy-start | bytes 2359300
  307.5 7.2 %copy-start = (f32[512,768]{1,0:T(8,128)S(1)}, f32[512,768]{1,0:T(8,128)}, u32[]{:S(2)}) copy-start(f32[512,768]{1,0:T(8,128)} %get-tuple-element.124) | copy-start | bytes 4718596
  307.5 8.3 %copy-start.4 = (f32[2,48,384]{2,1,0:T(8,128)S(1)}, f32[2,48,384]{2,1,0:T(8,128)}, u32[]{:S(2)}) copy-start(f32[2,48,384]{2,1,0:T(8,128)} %get-tuple-element.74) | copy-start | bytes 442372
  311.9 5.4 %copy-start.2 = (f32[2,48,1536]{2,1,0:T(8,128)S(1)}, f32[2,48,1536]{2,1,0:T(8,128)}, u32[]{:S(2)}) copy-start(f32[2,48,1536]{2,1,0:T(8,128)} %get-tuple-element.76) | copy-start | bytes 1769476
  313.8 2.7 copy-start.3
where the time goes:
time: 318 us
  Pallas kernels  300 us (94%)
  local copies, waits for them, and re-layouts  17.8 us (6%)
    pallas_call x1, Pallas kernels, backward(): pl.pallas_call(backward_kernel, out_shape=[jax.ShapeDtypeStruct((2, 48, w...  160 us
    pallas_call x1, Pallas kernels, forward(): pl.pallas_call(forward_kernel, out_shape=out_shape, in_specs=[any_spec] *...  139 us

commit v1 on v0

--- a/solution.py
+++ b/solution.py
@@ -15,56 +15,69 @@
 F32 = jnp.float32
 ITEM_COUNT = 8
 GATHER_CHAINS = (
-    (0, 0, 512, "zxy"),
-    (0, 512, 640, "zyx"),
-    (1, 0, 256, "yzx"),
-    (1, 256, 128, "xzy"),
-    (2, 0, 768, "zxy"),
-    (2, 768, 768, "zyx"),
-    (3, 0, 768, "zxy"),
-    (3, 768, 768, "zyx"),
-    (4, 0, 512, "xzy"),
-    (4, 512, 640, "yzx"),
-    (5, 0, 256, "zyx"),
-    (5, 256, 128, "zxy"),
-    (6, 0, 768, "zxy"),
-    (6, 768, 768, "zyx"),
-    (7, 0, 768, "xzy"),
-    (7, 768, 768, "yzx"),
+    (0, 0, 256, "zxy"),
+    (0, 256, 256, "zyx"),
+    (0, 512, 384, "zxy"),
+    (0, 896, 256, "zyx"),
+    (1, 0, 256, "zyx"),
+    (1, 256, 128, "zxy"),
+    (2, 0, 384, "zxy"),
+    (2, 384, 384, "zyx"),
+    (2, 768, 384, "zxy"),
+    (2, 1152, 384, "zyx"),
+    (3, 0, 384, "xzy"),
+    (3, 384, 384, "yzx"),
+    (3, 768, 384, "xzy"),
+    (3, 1152, 384, "yzx"),
+    (4, 0, 256, "zxy"),
+    (4, 256, 256, "zyx"),
+    (4, 512, 384, "zxy"),
+    (4, 896, 256, "zyx"),
+    (5, 0, 256, "yzx"),
+    (5, 256, 128, "xzy"),
+    (6, 0, 384, "zxy"),
+    (6, 384, 384, "zyx"),
+    (6, 768, 384, "xzy"),
+    (6, 1152, 384, "yzx"),
+    (7, 0, 384, "zxy"),
+    (7, 384, 384, "zyx"),
+    (7, 768, 384, "xzy"),
+    (7, 1152, 384, "yzx"),
 )
 GATHER_TABLE = (
-    (12, 32, 8, 36, 20, 0),
+    (80, 96, 152, 88, 104, 144, 8, 24, 0),
     (),
-    (-13, 56, -9, 60, -33, -37, -57, -61, -21, 21, 24, -1, 1, 13, -22, 22, -2, 2, -25, 25, 4, -14, 14, 16, -5, 44, -3, 5, 3, -15, 15, -23, -4, 23, -17, 17, 28, -16, -45, 9, -24, -6, -26, 6, 26, -29, 29, 40, -18, 45, -10, 33, -41, 37, -27, 18, 27, -7, 10, 7, -28, -34, 48, -46, -8, -30, 30, 46),
-    (-11, 11),
-    (-12,),
-    (-38, 38, 52),
-    (-19, 41, 19, -49, 57, -47, 34, 47, -31, 49),
-    (-20, 31, -48, -42),
-    (-32, -53, 53, 61),
+    (-81, 176, -89, 184, -97, 208, -105, 216, -153, -9, 16, -145, 9, -25, 32, -177, -185, 25, -209, -217, -1, 1, 40, -10, 10, -17, 17, 48, -26, -2, 26, 2, -33, 33, 72, -41, 64, -11, 41, 11, -49, 56, -3, 3, -12, -18, 49, 18, -73, 73, 81, -34, -4, -65, 89, -27, 34, 27, -42, 65, 42, -28, -57, 97, -50, -19, 50, 19, -20, -74, 74, 57),
+    (-35, 35, -82, 105, -43, 82, 43),
+    (-66, -36, -44),
+    (-90, 90, 112, -51, 66, 51, -75, 75),
+    (-58, 58, -52, -76, -98, 98, 120),
+    (-83, 83, -91, 91),
+    (-84, -106, 106, 128, -92, -113, 113, 136, -67, 67, -59, 59, -121, 121, 153, -68, -60, -129, 129, 145),
+    (-137, 137, 160, -99, 99, -107, 107, -154, 154, 168, -122, 122, -114, 114),
+    (-100, -108, -138, 138, -130, 130, -146, 146, 177, -155, 155),
+    (-161, 185, -156, -123, 161, 123, -115, 115, -169, 169, 192),
+    (-124, -139, 139, -116, -131, 131, -140, -147, 147, -178, 178, 200, -132, -170, 170, -148, -162, 162),
     (),
-    (-39, 42, 39, -35, 35),
-    (-40,),
-    (-36, -50, 50, -54, 54, -58, 58),
-    (-43, 43),
-    (-44,),
+    (-186, 186, 209),
+    (-179, 179, -193, 193, 217, -171, 171, -201, 201),
+    (-163, 163, -180, -172, -187, 187, -202, 202, -210, 210),
+    (-194, 194, -164, -188),
     (),
-    (-62, 62, -51, 51),
-    (-55, 55),
-    (-52, -56),
-    (),
-    (-59, 59, -63, 63, -60, -64),
-    (),
+    (-218, 218, -203, 203, -211, 211),
+    (-204, -212),
+    (-195, 195, -219, 219),
+    (-196, -220),
 )
 
 
 REDUCE_CHAINS = (
-    (0, 0, 768, "yzx"),
-    (0, 768, 768, "xzy"),
+    (0, 0, 768, "yxz"),
+    (0, 768, 768, "xyz"),
     (1, 0, 768, "yxz"),
     (1, 768, 768, "xyz"),
-    (2, 0, 256, "xzy"),
-    (2, 256, 128, "yzx"),
+    (2, 0, 256, "xyz"),
+    (2, 256, 128, "yxz"),
     (3, 0, 512, "yxz"),
     (3, 512, 640, "xyz"),
     (4, 0, 768, "yzx"),
@@ -78,32 +91,31 @@
 )
 REDUCE_TABLE = (
     (),
+    (8, 0),
     (),
     (),
     (),
-    (),
-    (4, 0),
-    (12, 8),
+    (24, 16, -1, 1, -9, 9),
     (),
     (),
-    (-1, 20, 1, -5, 16, 5),
+    (32, 40),
+    (-17, -25, 17, 25),
+    (-2, 2, -10, 10, -41, 41, -33, 33),
+    (56, 48, -26, 26),
+    (-18, -34, -42, -3, 42),
+    (-11, 18),
+    (-49, 49),
+    (-57, 57, -27, 34),
+    (72, 64, -43, -50, 50, -58, -19, 58),
+    (88, 80, -35, -51),
+    (-59, -65, 65, -73, 73),
     (),
-    (),
-    (-9, 24, -13, 9, -21, 13),
-    (-2, 21, -17, 2),
-    (),
-    (-10, 28, -25, -3, 25, -6, 6, 10, -22, 17, -14, -7),
-    (-29, 22, 29, -11, 14),
-    (32, -26, 36, -23, -18, 26, -30, 18, -15, 30),
-    (44, -27),
-    (-33, 40, 33, -37, -19, -31, 37),
-    (),
-    (48, 52),
-    (-45,),
-    (-34, 34, -41, 45, -49, 41, -53, 49),
-    (-35, 53),
-    (-46, 56, 46, -42, 60, -50, -54, -38, 38, 54),
-    (-47, 50, -55, 42, -57, 57, -39, -51, -61, 61, -58, 58, -43, -62, 62, -59, -63),
+    (96, 104),
+    (-81, 81, -89, 89),
+    (-105, 105, -66, -97, 66, 97),
+    (112, 128, -90, 90, -82, 120, 82, -98, -106, -129, 129),
+    (-67, -74, 74, 98),
+    (136, -113, 113, -91, 106, -75, -137, -121, 137, 121, -130, 130, -83, -114, 114, -138, 138, -99, -122, 122, -107, -131, 131, -139, -115, 139, -123, -132, 132, -140, -133),
 )
 
 
@@ -161,12 +173,12 @@
 
     def act(self, code):
         if code >= 0:
-            key = divmod(code, 4)
+            key = divmod(code, 8)
             self.live[key] = self.copies(*key)
             for copy in self.live[key]:
                 copy.start()
         else:
-            key = divmod(-code - 1, 4)
+            key = divmod(-code - 1, 8)
             for copy in self.live.pop(key):
                 copy.wait()
             self.arrived(*key)
@@ -181,15 +193,31 @@
     return slice(None) if axis in order[:count] else own
 
 
-def gather_chains(own, held, send, recv, local, peers, place):
+def gather_chains(shards, held, send, recv, local, peers, place):
     z, x, k, y = place
-    mine = {i: pltpu.make_async_copy(own[i], held[i].at[y, z, x, k], local.at[i]) for i in range(len(held))}
-    for copy in mine.values():
-        copy.start()
+    mine = {}
+    for layer in range(2):
+        for kind in range(4):
+            i = 4 * layer + kind
+            target = held[i].at[y, z, x, k]
+            if kind == 0:
+                mine[i] = [
+                    pltpu.make_async_copy(shards[0].at[layer, t], target.at[:, pl.ds(t * 384, 384)], local.at[i, t])
+                    for t in range(3)
+                ]
+            else:
+                mine[i] = [pltpu.make_async_copy(shards[kind].at[layer], target, local.at[i, 0])]
+            for copy in mine[i]:
+                copy.start()
+
+    def put(i):
+        for copy in mine.pop(i, ()):
+            copy.wait()
 
     def copies(c, phase):
         i, first, width, order = GATHER_CHAINS[c]
         b, cols = held[i], pl.ds(first, width)
+        put(i)
 
         def remote(source, target, slot, peer):
             return pltpu.make_async_remote_copy(
@@ -201,15 +229,9 @@
             return [remote(ref, ref, 5, 5)]
         at = [axis_index_of(axis, own_at, order, phase) for axis, own_at in (("y", y), ("z", z), ("x", x))]
         target = b.at[(*at, k, slice(None), cols)]
-        if phase == 0:
-            source = own[i].at[:, cols]
-        else:
-            if i in mine:
-                mine.pop(i).wait()
-            source = target
         if order[phase] == "z":
-            return [remote(source, target, j, j) for j in range(3)]
-        return [remote(source, target, 3, 3) if order[phase] == "x" else remote(source, target, 4, 4)]
+            return [remote(target, target, j, j) for j in range(3)]
+        return [remote(target, target, 3, 3) if order[phase] == "x" else remote(target, target, 4, 4)]
 
     return Chains(GATHER_TABLE, copies, lambda c, phase: None)
 
@@ -243,17 +265,18 @@
     def take(count):
         return [next(it) for _ in range(count)]
 
-    own = take(n)
-    tokens, lengths, gain, shift, outb, qvb, upb = take(7)
+    shards = take(4)
+    tokens, cotangent, lengths, gain, shift, outb, qvb, upb = take(8)
     whole = take(n)
     saved = [take(9) for _ in range(2)]
-    (final,) = take(1)
+    (first_grad,) = take(1)
     held = take(n)
     (stream, middle, normed, turned, turned_mid, project, attended, active, slope, probs, qv_all, up_all) = take(12)
-    send, recv, local, out_sem, prob_sem, small_send, small_recv, whole_sem = take(8)
+    (grad, to_core, from_core) = take(3)
+    send, recv, local, out_sem, core_send, core_recv, small_send, small_recv, whole_sem, grad_sem = take(10)
     place = z, x, k, y = places()
     peers = partners(z, x, k, y)
-    chains = gather_chains(own, held, send, recv, local, peers, place)
+    chains = gather_chains(shards, held, send, recv, local, peers, place)
     qv_all[y] = qvb[...]
     up_all[y] = upb[...]
     greet(peers)
@@ -387,7 +410,9 @@
         save(layer, 7, active)
         save(layer, 8, slope)
         chains.at()
-        keep_weight(4 * layer + 3)
+        if layer == 1:
+            break
+        keep_weight(3)
         settle(0)
 
         def close(c, carry):
@@ -399,17 +424,54 @@
             return carry
 
         lax.fori_loop(0, 2, close, 0)
+
+    keep = lax.broadcasted_iota(jnp.int32, (rows, 1), 0) < length
+    normed[...] = jnp.where(keep, cotangent[...], jnp.zeros_like(cotangent[...]))
+    settle(2)
+    turn_rows(normed, turned, k)
+    def across(half):
+        return pltpu.make_async_remote_copy(
+            to_core.at[half], from_core.at[half], core_send.at[half], core_recv.at[half],
+            device_id=peers[5], device_id_type=MESH,
+        )
+
+    def first_half(half, carry):
+        def chunk(t, inner):
+            cols = pl.ds(pl.multiple_of(t * 512, 128), 512)
+            value = mm(turned[...].reshape(768, rows), active[half, :, cols], ((1,), (0,))).astype(BF16)
+            grad[half, :, :, :, cols] = value[:384].reshape(4, 2, 48, 512)
+            to_core[half, :, :, :, cols] = value[384:].reshape(4, 2, 48, 512)
+            return inner
+
+        lax.fori_loop(0, 3, chunk, 0)
+        across(half).start()
+        return carry
+
+    lax.fori_loop(0, 2, first_half, 0)
     chains.at()
-    final[...] = stream[...].astype(BF16)
+    for half in range(2):
+        across(half).wait()
+
+    def join(t, carry):
+        at = (t // 8, (t // 2) % 4, t % 2)
+        grad[at] = grad[at] + from_core[at]
+        return carry
+
+    lax.fori_loop(0, 16, join, 0)
+    back.append(pltpu.make_async_copy(grad, first_grad, grad_sem))
+    back[-1].start()
+    chains.at()
+    keep_weight(7)
     for slot in list(outgoing):
         settle(slot)
     for copy in back:
         copy.wait()
 
 
-def forward(shards, tokens, lengths, gain, shift, outb, qvb, upb):
+def forward(shards, tokens, cotangent, lengths, gain, shift, outb, qvb, upb):
     rows, width = tokens.shape
-    widths = [s.shape[-1] for s in shards]
+    qkv, out, up, down = shards
+    widths = [3 * qkv.shape[3], out.shape[2], up.shape[2], down.shape[2]] * 2
     full = [(2, 4, 2, 2, 48, w) for w in widths]
     layer_saves = [
         ((rows, width), F32),
@@ -427,14 +489,14 @@
     out_shape = (
         [jax.ShapeDtypeStruct(f, BF16) for f in full]
         + [jax.ShapeDtypeStruct(s, t) for s, t in layer_saves * 2]
-        + [jax.ShapeDtypeStruct((rows, width), BF16)]
+        + [jax.ShapeDtypeStruct((2, 4, 2, 48, widths[3]), BF16)]
     )
     by_slot = {j: pltpu.VMEM(*layer_saves[j]) for j in range(9)}
     outs = pl.pallas_call(
         forward_kernel,
         out_shape=out_shape,
-        in_specs=[any_spec] * ITEM_COUNT + [vmem_spec, pl.BlockSpec(memory_space=pltpu.SMEM)] + [vmem_spec] * 5,
-        out_specs=[any_spec] * (ITEM_COUNT + 18) + [vmem_spec],
+        in_specs=[any_spec] * 4 + [vmem_spec] * 2 + [pl.BlockSpec(memory_space=pltpu.SMEM)] + [vmem_spec] * 5,
+        out_specs=[any_spec] * (ITEM_COUNT + 19),
         scratch_shapes=[pltpu.VMEM(f, BF16) for f in full]
         + [
             by_slot[0],
@@ -449,20 +511,25 @@
             by_slot[6],
             pltpu.VMEM((2, *qvb.shape), F32),
             pltpu.VMEM((2, *upb.shape), F32),
+            pltpu.VMEM((2, 4, 2, 48, widths[3]), BF16),
+            pltpu.VMEM((2, 4, 2, 48, widths[3]), BF16),
+            pltpu.VMEM((2, 4, 2, 48, widths[3]), BF16),
             pltpu.SemaphoreType.DMA((len(GATHER_CHAINS), 6)),
             pltpu.SemaphoreType.DMA((len(GATHER_CHAINS), 6)),
-            pltpu.SemaphoreType.DMA((ITEM_COUNT,)),
+            pltpu.SemaphoreType.DMA((ITEM_COUNT, 3)),
             pltpu.SemaphoreType.DMA((2, 9)),
             pltpu.SemaphoreType.DMA((2,)),
             pltpu.SemaphoreType.DMA((2,)),
             pltpu.SemaphoreType.DMA((2,)),
+            pltpu.SemaphoreType.DMA((2,)),
             pltpu.SemaphoreType.DMA((ITEM_COUNT,)),
+            pltpu.SemaphoreType.DMA,
         ],
         compiler_params=pltpu.CompilerParams(
             collective_id=0, has_side_effects=True, vmem_limit_bytes=VMEM_LIMIT
         ),
         name="forward",
-    )(*shards, tokens, lengths, gain, shift, outb, qvb, upb)
+    )(*shards, tokens, cotangent, lengths, gain, shift, outb, qvb, upb)
     return outs[:ITEM_COUNT], [outs[ITEM_COUNT + 9 * l : ITEM_COUNT + 9 * l + 9] for l in range(2)], outs[-1]
 
 
@@ -499,16 +566,16 @@
 
     whole = take(n)
     saved = [take(9) for _ in range(2)]
-    cotangent, lengths, gain = take(3)
-    out_q, out_o, out_u, out_d, token_grad, sums = take(6)
+    first_grad, cotangent, lengths, gain, outb = take(5)
+    out_q, out_o, out_u, out_d, token_grad, sums, late, final = take(8)
     outs = (out_q, out_o, out_u, out_d)
     (slot_a, slot_b, stream, middle, turned, turned_mid, project, attended, active, slope, probs) = take(11)
     (gradient, upstream, rounded, left, dattended, dproject) = take(6)
     held = take(4)
     (to_core, from_core) = take(2)
     arrivals = [take(3) for _ in REDUCE_CHAINS]
-    small_c, small_x, small_y, small_z = take(4)
-    (fetch_sem, prob_sem, core_send, core_recv, send, recv, credit, small_send, small_recv, last_sem) = take(10)
+    small_c, small_x, small_y, small_b, small_z, late_in, late_z = take(7)
+    (fetch_sem, prob_sem, core_send, core_recv, send, recv, credit, small_send, small_recv, last_sem, final_sem) = take(11)
     place = z, x, k, y = places()
     peers = partners(z, x, k, y)
     rows = stream.shape[0]
@@ -533,7 +600,7 @@
         lead = (slice(None),) * 5
         return [(w_qkv, slot.at[(*lead, pl.ds(0, 1152))]), (w_out, slot.at[(*lead, pl.ds(1152, 384))])]
 
-    SLOT_A, SLOT_B, STREAM, MIDDLE, TURNED, TURNED_MID, PROJECT, ATTENDED, ACTIVE, SLOPE, COT = range(11)
+    SLOT_A, SLOT_B, STREAM, MIDDLE, TURNED, TURNED_MID, PROJECT, ATTENDED, ACTIVE, SLOPE, COT, GRAD = range(12)
     buffers = {
         STREAM: (stream, 0),
         MIDDLE: (middle, 1),
@@ -552,12 +619,13 @@
     def prob_copy(layer, j):
         return pltpu.make_async_copy(saved[layer][6].at[j], probs.at[j % 2], prob_sem.at[j % 2])
 
+    fetch(GRAD, [(first_grad, held[3])])
     fetch(COT, [(cotangent, rounded)])
     fetch(SLOT_A, weights_into(slot_a, 1, "d"))
-    for name in (SLOPE, ACTIVE):
+    for name in (SLOPE, ACTIVE, MIDDLE, TURNED_MID):
         fetch_saved(name, 1)
     fetch(SLOT_B, weights_into(slot_b, 1, "u"))
-    for name in (TURNED_MID, MIDDLE, ATTENDED, PROJECT, TURNED, STREAM):
+    for name in (ATTENDED, PROJECT, TURNED, STREAM):
         fetch_saved(name, 1)
     prob_copy(1, 0).start()
     slots = {("d", 1): (SLOT_A, slot_a), ("u", 1): (SLOT_B, slot_b), ("q", 1): (SLOT_A, slot_a),
@@ -652,7 +720,47 @@
 
             lax.fori_loop(0, count, block, 0)
 
-    chains = Chains(REDUCE_TABLE, copies, arrived)
+    early, late_at = len(REDUCE_CHAINS), len(REDUCE_CHAINS) + 1
+
+    def small_copies(c, phase):
+        def remote(source, target, slot, peer):
+            return pltpu.make_async_remote_copy(
+                source, target, small_send.at[slot], small_recv.at[slot], device_id=peers[peer], device_id_type=MESH
+            )
+
+        if c == early:
+            if phase == 0:
+                return [remote(sums.at[1 - k], small_c, 0, 5)]
+            if phase == 3:
+                small_z[z] = sums[k]
+                return [remote(sums.at[k], small_z.at[z], 3 + j, j) for j in range(3)]
+            target, slot, peer = ((small_x, 1, 3), (small_y, 2, 4), None, (small_b, 6, 5))[phase - 1]
+            return [remote(sums.at[k], target, slot, peer)]
+        if phase == 3:
+            late_z[z] = late[...]
+            return [remote(late, late_z.at[z], 10 + j, j) for j in range(3)]
+        return [remote(late, late_in.at[phase], 7 + phase, (5, 3, 4)[phase])]
+
+    def small_arrived(c, phase):
+        if c == early:
+            if phase == 4:
+                sums[1 - k] = small_b[...]
+            elif phase == 3:
+                sums[k] = (small_z[0] + small_z[1]) + (small_z[2] + small_z[3])
+            else:
+                sums[k] += (small_c, small_x, small_y)[phase][...]
+        elif phase == 3:
+            late[...] = (late_z[0] + late_z[1]) + (late_z[2] + late_z[3])
+        else:
+            late[...] += late_in[phase]
+
+    def any_copies(c, phase):
+        return copies(c, phase) if c < early else small_copies(c, phase)
+
+    def any_arrived(c, phase):
+        return arrived(c, phase) if c < early else small_arrived(c, phase)
+
+    chains = Chains(REDUCE_TABLE, any_copies, any_arrived)
 
     def weight_gradient(r, lhs, rhs):
         b = held[kinds[r][1]]
@@ -668,14 +776,17 @@
                 return inner
 
             lax.fori_loop(0, width // size, chunk, 0)
-            if r > 0:
+            if r > 1:
                 pl.semaphore_wait(credit.at[half], 1)
             core_copy(r, half).start()
             return carry
 
         lax.fori_loop(0, 2, one, 0)
 
+    sums[0, 0:2, 0:768] = jnp.zeros((2, 768), F32)
+    sums[:, 6:8, :] = jnp.zeros((2, 2, 1536), F32)
     chains.at()
+    ready(GRAD)
     chains.at()
     ready(COT)
     keep = lax.broadcasted_iota(jnp.int32, (rows, 1), 0) < lengths[y]
@@ -692,11 +803,12 @@
         first = 0 if layer == 1 else 4
         place_at()
         sums[layer, 2:3, 768:1536] = jnp.sum(gradient[...], axis=0, keepdims=True)
-        turn_rows(rounded, left, k)
         name, w_down = slots["d", layer]
-        ready(ACTIVE)
-        place_at()
-        weight_gradient(first, left, lambda half, cols: active[half, :, cols])
+        if layer == 0:
+            turn_rows(rounded, left, k)
+            ready(ACTIVE)
+            place_at()
+            weight_gradient(first, left, lambda half, cols: active[half, :, cols])
         ready(name)
         ready(SLOPE)
         place_at()
@@ -712,6 +824,24 @@
 
         lax.fori_loop(0, 6, unit, 0)
         if layer == 1:
+            ready(ACTIVE)
+            ready(MIDDLE)
+
+            def close(c, carry):
+                cols = pl.ds(pl.multiple_of(c * 384, 128), 384)
+                total = middle[:, cols] + outb[1, 1:2, cols]
+                for half in range(2):
+                    total += mm(active[half], matrix(w_down, half, pl.ds(2 * c, 2)), ((1,), (1,)))
+                dattended[c] = total.astype(BF16)
+                return carry
+
+            lax.fori_loop(0, 2, close, 0)
+            finals = [
+                pltpu.make_async_copy(dattended.at[c], final.at[:, pl.ds(c * 384, 384)], final_sem.at[c])
+                for c in range(2)
+            ]
+            for copy in finals:
+                copy.start()
             fetch(SLOT_A, weights_into(slot_a, 1, "q"))
             fetch_saved(ACTIVE, 0)
         else:
@@ -719,7 +849,7 @@
         name, w_up = slots["u", layer]
         ready(name)
         ready(TURNED_MID)
-        place_at(first)
+        place_at(*([first] if first else []))
         weight_gradient(first + 1, turned_mid, lambda half, cols: slope[half, :, cols])
         place_at(first + 1)
 
@@ -734,7 +864,8 @@
             fetch(SLOT_B, weights_into(slot_b, 0, "d"))
             fetch_saved(SLOPE, 0)
             fetch_saved(TURNED_MID, 0)
-        ready(MIDDLE)
+        if layer == 0:
+            ready(MIDDLE)
         place_at()
         gain_sum, shift_sum, bias_sum = norm_back(middle, upstream, gain[layer, 1:2], gradient, rounded)
         sums[layer, 0:1, 768:1536] = gain_sum
@@ -748,6 +879,10 @@
         place_at()
         turn_rows(rounded, left, k)
         weight_gradient(first + 2, left, lambda half, cols: attended[:, pl.ds(pl.multiple_of(half * 384, 128), 384)])
+
+        if layer == 1:
+            for copy in finals:
+                copy.wait()
 
         def pull_out(half, carry):
             dattended[half] = mm(rounded[...], matrix(w_qo, half, *everything, pl.ds(1152, 384)), ((1,), (0,))).astype(BF16)
@@ -820,41 +955,21 @@
         ready(STREAM)
         place_at()
         gain_sum, shift_sum, _ = norm_back(stream, upstream, gain[layer, 0:1], gradient, rounded if layer == 1 else None)
-        sums[layer, 0:1, 0:768] = gain_sum
-        sums[layer, 1:2, 0:768] = shift_sum
         if layer == 1:
+            sums[1, 0:1, 0:768] = gain_sum
+            sums[1, 1:2, 0:768] = shift_sum
             fetch_saved(STREAM, 0)
+        else:
+            late[0:1] = gain_sum
+            late[1:2] = shift_sum
     last = pltpu.make_async_copy(gradient, token_grad, last_sem)
     last.start()
 
-    sums[:, 6:8, :] = jnp.zeros((2, 2, 1536), F32)
-
-    def exchange(slot, target, peer):
-        copy = pltpu.make_async_remote_copy(
-            sums, target, small_send.at[slot], small_recv.at[slot], device_id=peers[peer], device_id_type=MESH
-        )
-        copy.start()
-        return copy
-
-    tail = chains.table[chains.spot]
-    parts = [tail[len(tail) * j // 4 : len(tail) * (j + 1) // 4] for j in range(4)]
-    for slot, (target, peer) in enumerate(((small_c, 5), (small_x, 3), (small_y, 4))):
-        copy = exchange(slot, target, peer)
-        for code in parts[slot]:
-            chains.act(code)
-        copy.wait()
-        sums[...] += target[...]
-    small_z[z] = sums[...]
-    across = [exchange(3 + j, small_z.at[z], j) for j in range(3)]
-    for code in parts[3]:
-        chains.act(code)
-    for copy in across:
-        copy.wait()
-    sums[...] = (small_z[0] + small_z[1]) + (small_z[2] + small_z[3])
+    chains.at()
     last.wait()
 
 
-def backward(whole, saved, cotangent, lengths, gain):
+def backward(whole, saved, first_grad, cotangent, lengths, gain, outb):
     rows, width = cotangent.shape
     widths = [w.shape[-1] for w in whole[:4]]
     any_spec = pl.BlockSpec(memory_space=pl.ANY)
@@ -877,9 +992,14 @@
     outs = pl.pallas_call(
         backward_kernel,
         out_shape=[jax.ShapeDtypeStruct((2, 48, w), F32) for w in widths]
-        + [jax.ShapeDtypeStruct((rows, width), F32), jax.ShapeDtypeStruct(small, F32)],
-        in_specs=[any_spec] * (ITEM_COUNT + 18 + 1) + [pl.BlockSpec(memory_space=pltpu.SMEM), vmem_spec],
-        out_specs=[vmem_spec] * 4 + [any_spec, vmem_spec],
+        + [
+            jax.ShapeDtypeStruct((rows, width), F32),
+            jax.ShapeDtypeStruct(small, F32),
+            jax.ShapeDtypeStruct((2, width), F32),
+            jax.ShapeDtypeStruct((rows, width), BF16),
+        ],
+        in_specs=[any_spec] * (ITEM_COUNT + 18 + 2) + [pl.BlockSpec(memory_space=pltpu.SMEM), vmem_spec, vmem_spec],
+        out_specs=[vmem_spec] * 4 + [any_spec, vmem_spec, vmem_spec, any_spec],
         scratch_shapes=[
             pltpu.VMEM((2, 4, 2, 2, 48, wide), BF16),
             pltpu.VMEM((2, 4, 2, 2, 48, wide), BF16),
@@ -902,25 +1022,26 @@
         + blocks(2, 4, 2)
         + [pltpu.VMEM((2, 4, 2, 48, wide), BF16), pltpu.VMEM((2, 4, 2, 48, wide), BF16)]
         + arrival_shapes()
-        + [pltpu.VMEM(small, F32)] * 3
-        + [pltpu.VMEM((4, *small), F32)]
+        + [pltpu.VMEM(small[1:], F32)] * 4
+        + [pltpu.VMEM((4, *small[1:]), F32), pltpu.VMEM((3, 2, width), F32), pltpu.VMEM((4, 2, width), F32)]
         + [
-            pltpu.SemaphoreType.DMA((11, 2)),
+            pltpu.SemaphoreType.DMA((12, 2)),
             pltpu.SemaphoreType.DMA((2,)),
             pltpu.SemaphoreType.DMA((ITEM_COUNT, 2)),
             pltpu.SemaphoreType.DMA((ITEM_COUNT, 2)),
             pltpu.SemaphoreType.DMA((len(REDUCE_CHAINS), 5)),
             pltpu.SemaphoreType.DMA((len(REDUCE_CHAINS), 5)),
             pltpu.SemaphoreType.REGULAR((2,)),
-            pltpu.SemaphoreType.DMA((6,)),
-            pltpu.SemaphoreType.DMA((6,)),
+            pltpu.SemaphoreType.DMA((13,)),
+            pltpu.SemaphoreType.DMA((13,)),
             pltpu.SemaphoreType.DMA,
+            pltpu.SemaphoreType.DMA((2,)),
         ],
         compiler_params=pltpu.CompilerParams(
             collective_id=1, has_side_effects=True, vmem_limit_bytes=63 * 2**20
         ),
         name="backward",
-    )(*whole, *saved[0], *saved[1], cotangent, lengths, gain)
+    )(*whole, *saved[0], *saved[1], first_grad, cotangent, lengths, gain, outb)
     return outs
 
 
@@ -1045,38 +1166,88 @@
     return (final, gradient, g_gain, g_shift, g_qkv, g_qvb, g_out, g_up, g_upb, g_down, g_outb)
 
 
+def finish_kernel(*refs):
+    g_qkv, g_out, g_up, g_down, token_grad, sums, late, final = refs[:8]
+    o_final, o_token, o_gain, o_shift, o_qkv, o_qvb, o_out, o_up, o_upb, o_down, o_outb = refs[8:19]
+    (sem,) = refs[19:]
+    y = lax.axis_index("tensor")
+    width = late.shape[1]
+    third = width // 2
+    pairs = [(token_grad, o_token), (final, o_final), (g_up, o_up), (g_out, o_out), (g_down, o_down)]
+    for layer in range(2):
+        for t in range(3):
+            pairs.append((g_qkv.at[layer, :, pl.ds(t * third, third)], o_qkv.at[layer, t]))
+    moves = [pltpu.make_async_copy(source, target, sem.at[j]) for j, (source, target) in enumerate(pairs)]
+    for copy in moves:
+        copy.start()
+    for layer in range(2):
+        o_upb[layer : layer + 1] = sums[layer, pl.ds(4 + y, 1)]
+        for j in range(2):
+            at = slice(j * width, (j + 1) * width)
+            here = pl.ds(pl.multiple_of(j * width + y * third, 128), third)
+            o_outb[layer, j : j + 1] = sums[layer, 2:3, at]
+            o_qvb[layer, j : j + 1] = sums[layer, 3:4, here]
+            if layer == 0 and j == 0:
+                o_gain[0, 0:1] = late[0:1]
+                o_shift[0, 0:1] = late[1:2]
+            else:
+                o_gain[layer, j : j + 1] = sums[layer, 0:1, at]
+                o_shift[layer, j : j + 1] = sums[layer, 1:2, at]
+    for copy in moves:
+        copy.wait()
+
+
 def fused_body(tokens, lengths, cotangent, norm_gain, norm_shift, qkv_weight, qv_bias, out_weight, up_weight,
                up_bias, down_weight, out_bias):
-    part = lax.axis_index("tensor")
-    layers = norm_gain.shape[0]
-    rows, width = tokens.shape
-    third = width // 2
-    own = qkv_weight.shape[1]
-    shards = []
-    for layer in range(layers):
-        shards += [
-            qkv_weight[layer].reshape(own, -1),
-            out_weight[layer].T,
-            up_weight[layer],
-            down_weight[layer].T,
-        ]
-    full, saved, final = forward(shards, tokens, lengths, norm_gain, norm_shift, out_bias, qv_bias, up_bias)
-    g_qkv, g_out, g_up, g_down, token_grad, small = backward(full, saved, cotangent, lengths, norm_gain)
-    g_gain, g_shift, g_outb, g_qvb = (small[:, j].reshape(layers, 2, width) for j in range(4))
-    g_upb = lax.dynamic_index_in_dim(small, 4 + part, axis=1, keepdims=False)
-    g_qvb = lax.dynamic_slice_in_dim(g_qvb, part * third, third, axis=2)
+    shards = (
+        qkv_weight.transpose(0, 2, 1, 3),
+        out_weight.transpose(0, 2, 1),
+        up_weight,
+        down_weight.transpose(0, 2, 1),
+    )
+    full, saved, first_grad = forward(
+        shards, tokens, cotangent, lengths, norm_gain, norm_shift, out_bias, qv_bias, up_bias
+    )
+    reduced = backward(full, saved, first_grad, cotangent, lengths, norm_gain, out_bias)
+    any_spec = pl.BlockSpec(memory_space=pl.ANY)
+    vmem_spec = pl.BlockSpec(memory_space=pltpu.VMEM)
+
+    def shape(array, kind=F32):
+        return jax.ShapeDtypeStruct(array.shape, kind)
+
+    outs = pl.pallas_call(
+        finish_kernel,
+        out_shape=(
+            shape(tokens, BF16),
+            shape(tokens),
+            shape(norm_gain),
+            shape(norm_shift),
+            shape(shards[0]),
+            shape(qv_bias),
+            shape(shards[1]),
+            shape(shards[2]),
+            shape(up_bias),
+            shape(shards[3]),
+            shape(out_bias),
+        ),
+        in_specs=[vmem_spec] * 8,
+        out_specs=(any_spec, any_spec, vmem_spec, vmem_spec, any_spec, vmem_spec, any_spec, any_spec, vmem_spec, any_spec, vmem_spec),
+        scratch_shapes=[pltpu.SemaphoreType.DMA((11,))],
+        name="finish",
+    )(*reduced)
+    final, token_grad, gain, shift, g_qkv, qvb, g_out, g_up, upb, g_down, outb = outs
     return (
         final,
         token_grad,
-        g_gain,
-        g_shift,
-        g_qkv.reshape(layers, own, 3, third),
-        g_qvb,
+        gain,
+        shift,
+        g_qkv.transpose(0, 2, 1, 3),
+        qvb,
         g_out.transpose(0, 2, 1),
         g_up,
-        g_upb,
+        upb,
         g_down.transpose(0, 2, 1),
-        g_outb,
+        outb,
     )
 
 

time: 318 us -> 295 us (0.928)
  local copies, waits for them, and re-layouts: 17.8 us -> 0 us
  Pallas kernels: 300 us -> 294 us
    unnamed x18 -> x0, local copies, waits for them, and re-layouts: 6.26 us -> none
    pallas_call x1, Pallas kernels: 160 us -> 154 us  [backward(): pl.pallas_call(backward_kernel, out_shape=[jax.ShapeDtypeStruct((2, 48, w...]
    pallas_call x0 -> x1, Pallas kernels: none -> 4.88 us  [fused_body(): pl.pallas_call(finish_kernel, out_shape=(shape(tokens, BF16), shape(token...]
    pallas_call x1, Pallas kernels: 139 us -> 135 us  [forward(): pl.pallas_call(forward_kernel, out_shape=out_shape, in_specs=[any_spec] *...]
where the time goes in v1:
time: 295 us
  Pallas kernels  294 us (100%)
    pallas_call x1, Pallas kernels, backward(): pl.pallas_call(backward_kernel, out_shape=[jax.ShapeDtypeStruct((2, 48, w...  154 us
    pallas_call x1, Pallas kernels, forward(): pl.pallas_call(forward_kernel, out_shape=out_shape, in_specs=[any_spec] *...  135 us

profile of v1, /device:TPU:0, one launch (start us, length us, event | category | flops | bytes accessed | tf_op | source)
XLA Modules:
  0.0 295.2 jit_solution(4920651713749772488)
XLA Ops:
  0.6 135.1 %forward.1 = (bf16[2,4,2,2,48,1152]{5,4,3,2,1,0:T(8,128)(2,1)}, bf16[2,4,2,2,48,384]{5,4,3,2,1,0:T(8,128)(2,1)}, bf16[2,4,2,2,48,1536]{5,4,3,2,1,0:T(8,128)(2,1)...) custom-call(bf16[2,3,48,384]{3,2,1,0:T(8,128)(2,1)} %bitcast.7, ...), custom_call_target="tpu_custom_call" | custom-call | tf_op jit(solution)/shard_map/forward/pallas_call | solution.py:495
  135.7 154.4 %backward.1 = (f32[2,48,1152]{2,1,0:T(8,128)}, f32[2,48,384]{2,1,0:T(8,128)}, f32[2,48,1536]{2,1,0:T(8,128)}, f32[2,48,1536]{2,1,0:T(8,128)}, f32[512,768]{1,0:T...) custom-call(bf16[2,4,2,2,48,1152]{5,4,3,2,1,0:T(8,128)(2,1)} %get-tuple-element.57.refs_0_, ...), custom_call_target="tpu_custom_call" | custom-call | tf_op jit(solution)/shard_map/backward/pallas_call | solution.py:992
  290.1 4.9 %finish.1 = (bf16[512,768]{1,0:T(8,128)(2,1)}, f32[512,768]{1,0:T(8,128)}, f32[2,2,768]{2,1,0:T(2,128)}, f32[2,2,768]{2,1,0:T(2,128)}, f32[2,3,48,384]{3,2,1,0:T...) custom-call(f32[2,48,1152]{2,1,0:T(8,128)} %get-tuple-element.84.ref, ...), custom_call_target="tpu_custom_call" | custom-call | tf_op jit(solution)/shard_map/finish/pallas_call | solution.py:1218

commit v2 on v1

--- a/solution.py
+++ b/solution.py
@@ -25,97 +25,108 @@
     (2, 384, 384, "zyx"),
     (2, 768, 384, "zxy"),
     (2, 1152, 384, "zyx"),
-    (3, 0, 384, "xzy"),
-    (3, 384, 384, "yzx"),
-    (3, 768, 384, "xzy"),
-    (3, 1152, 384, "yzx"),
-    (4, 0, 256, "zxy"),
-    (4, 256, 256, "zyx"),
+    (3, 0, 384, "zxy"),
+    (3, 384, 384, "zyx"),
+    (3, 768, 384, "zxy"),
+    (3, 1152, 384, "zyx"),
+    (4, 0, 256, "xyz"),
+    (4, 256, 256, "yxz"),
     (4, 512, 384, "zxy"),
     (4, 896, 256, "zyx"),
-    (5, 0, 256, "yzx"),
-    (5, 256, 128, "xzy"),
-    (6, 0, 384, "zxy"),
-    (6, 384, 384, "zyx"),
-    (6, 768, 384, "xzy"),
-    (6, 1152, 384, "yzx"),
+    (5, 0, 256, "zyx"),
+    (5, 256, 128, "zxy"),
+    (6, 0, 384, "xzy"),
+    (6, 384, 384, "yzx"),
+    (6, 768, 384, "zxy"),
+    (6, 1152, 384, "zyx"),
     (7, 0, 384, "zxy"),
     (7, 384, 384, "zyx"),
-    (7, 768, 384, "xzy"),
-    (7, 1152, 384, "yzx"),
+    (7, 768, 384, "zxy"),
+    (7, 1152, 384, "zyx"),
 )
 GATHER_TABLE = (
-    (80, 96, 152, 88, 104, 144, 8, 24, 0),
+    (112, 160, 168, 120, 40, 48, 24, 8),
     (),
-    (-81, 176, -89, 184, -97, 208, -105, 216, -153, -9, 16, -145, 9, -25, 32, -177, -185, 25, -209, -217, -1, 1, 40, -10, 10, -17, 17, 48, -26, -2, 26, 2, -33, 33, 72, -41, 64, -11, 41, 11, -49, 56, -3, 3, -12, -18, 49, 18, -73, 73, 81, -34, -4, -65, 89, -27, 34, 27, -42, 65, 42, -28, -57, 97, -50, -19, 50, 19, -20, -74, 74, 57),
-    (-35, 35, -82, 105, -43, 82, 43),
-    (-66, -36, -44),
-    (-90, 90, 112, -51, 66, 51, -75, 75),
-    (-58, 58, -52, -76, -98, 98, 120),
-    (-83, 83, -91, 91),
-    (-84, -106, 106, 128, -92, -113, 113, 136, -67, 67, -59, 59, -121, 121, 153, -68, -60, -129, 129, 145),
-    (-137, 137, 160, -99, 99, -107, 107, -154, 154, 168, -122, 122, -114, 114),
-    (-100, -108, -138, 138, -130, 130, -146, 146, 177, -155, 155),
-    (-161, 185, -156, -123, 161, 123, -115, 115, -169, 169, 192),
-    (-124, -139, 139, -116, -131, 131, -140, -147, 147, -178, 178, 200, -132, -170, 170, -148, -162, 162),
+    (-113, 113, -169, -41, 41, 0, -121, 121, -161, -49, 49, 16, -114, -42, 42, -25, 25, 32, -122, -9, 9, 80, -50, 50, -43, 43, -1, 1, 56, -26, 26, -44, -17, 17, 72, -10, 10, -2, 2, -33, 33, 144, -81, 81, 88, -27, 27, -51, 51, -28, -57, 57, 64, -18, 18, -52, -3, 3, -73, 73, 104, -11, 11, -34, 34, -4, -145, 145, 96, -12, -82, -58, 58, 82, -89, 176, -65, 65, 136, -35, 35, -19, 89, 19, -36, -105, 128, -20),
+    (-74, 74, 105, -97, 97, 152, -59, 59, -146, 146),
+    (-177, 114, -66, 177, 66),
+    (-60, -137, 169, -83, 137, 83, -129, 192, -153, 184, -75, 129, 75, -90, -98, 90, 98, -106),
     (),
-    (-186, 186, 209),
-    (-179, 179, -193, 193, 217, -171, 171, -201, 201),
-    (-163, 163, -180, -172, -187, 187, -202, 202, -210, 210),
-    (-194, 194, -164, -188),
+    (-84, -76, -147, 106, 147, -115, 122, 115, -67, 67, -178, 153, 178, -148, -116, -138, -68),
+    (-130, 138, 130, -170, 216),
+    (-193, 161, -99, 99, -91, 170, 91, -185, 185, 200, -100, -92, -179, 179, -107, 193, 107, -154, 154, -180, -108, -123, 208, 123),
+    (-131, 131, -139, 139, -124, -217, 217),
+    (-186, 186, -132, -140),
+    (-155, 155, -171, 171),
+    (-162, 162, -218, 218, -156, -194, 194),
+    (-172, -201, 201, -209, 209, -187, 187, -163, 163),
     (),
-    (-218, 218, -203, 203, -211, 211),
-    (-204, -212),
-    (-195, 195, -219, 219),
-    (-196, -220),
+    (-188, -219, 219, -164),
+    (-195, 195, -210, 210, -220, -202, 202),
+    (-196,),
+    (-211, 211, -203, 203),
+    (-212, -204),
 )
 
 
 REDUCE_CHAINS = (
-    (0, 0, 768, "yxz"),
-    (0, 768, 768, "xyz"),
-    (1, 0, 768, "yxz"),
-    (1, 768, 768, "xyz"),
+    (0, 0, 384, "yxz"),
+    (0, 384, 384, "xyz"),
+    (0, 768, 384, "yzx"),
+    (0, 1152, 384, "xzy"),
+    (1, 0, 384, "yxz"),
+    (1, 384, 384, "xyz"),
+    (1, 768, 384, "yzx"),
+    (1, 1152, 384, "xzy"),
     (2, 0, 256, "xyz"),
     (2, 256, 128, "yxz"),
-    (3, 0, 512, "yxz"),
-    (3, 512, 640, "xyz"),
-    (4, 0, 768, "yzx"),
-    (4, 768, 768, "xzy"),
-    (5, 0, 768, "yxz"),
-    (5, 768, 768, "xyz"),
+    (3, 0, 256, "yxz"),
+    (3, 256, 256, "xyz"),
+    (3, 512, 384, "yxz"),
+    (3, 896, 256, "xyz"),
+    (4, 0, 384, "yxz"),
+    (4, 384, 384, "xyz"),
+    (4, 768, 384, "yzx"),
+    (4, 1152, 384, "xzy"),
+    (5, 0, 384, "yxz"),
+    (5, 384, 384, "xyz"),
+    (5, 768, 384, "yxz"),
+    (5, 1152, 384, "xyz"),
     (6, 0, 256, "xyz"),
     (6, 256, 128, "yxz"),
-    (7, 0, 512, "yxz"),
-    (7, 512, 640, "xyz"),
+    (7, 0, 256, "yxz"),
+    (7, 256, 256, "xyz"),
+    (7, 512, 384, "yxz"),
+    (7, 896, 256, "xyz"),
 )
 REDUCE_TABLE = (
     (),
-    (8, 0),
+    (8, 24, 16, 0),
     (),
     (),
     (),
-    (24, 16, -1, 1, -9, 9),
+    (56, 32, -9, 40, -17, 48, 17),
+    (-1, 9, -25, 1, 25),
     (),
+    (-18, -33, 72, -57, 18, 57),
+    (-26, -41, 33, -49, 41, 49),
+    (-2, 64, 2, -10, 26, -19),
+    (104, -73, 80, -58, 10, -34, 73, -42, 58, -27, 96),
+    (-65, 88, -50, 34, -3, 42),
+    (-81, 65, -105, 81, -59, 105, -74, 50),
+    (-11, 74),
+    (-35, -89, 136, -97, 128),
+    (-82, 97, 82, -43, -66, 112, 66, -51, 120, -75, -106, 89, 106),
+    (-137, 152, -129, 144, -83, 137),
+    (-98, 168, -67, 129, -107, 98, -113, 160, -90, -121, 113, 121),
     (),
-    (32, 40),
-    (-17, -25, 17, 25),
-    (-2, 2, -10, 10, -41, 41, -33, 33),
-    (56, 48, -26, 26),
-    (-18, -34, -42, -3, 42),
-    (-11, 18),
-    (-49, 49),
-    (-57, 57, -27, 34),
-    (72, 64, -43, -50, 50, -58, -19, 58),
-    (88, 80, -35, -51),
-    (-59, -65, 65, -73, 73),
-    (),
-    (96, 104),
-    (-81, 81, -89, 89),
-    (-105, 105, -66, -97, 66, 97),
-    (112, 128, -90, 90, -82, 120, 82, -98, -106, -129, 129),
-    (-67, -74, 74, 98),
-    (136, -113, 113, -91, 106, -75, -137, -121, 137, 121, -130, 130, -83, -114, 114, -138, 138, -99, -122, 122, -107, -131, 131, -139, -115, 139, -123, -132, 132, -140, -133),
+    (-138, 90, -145, 184),
+    (-153, 145, -130),
+    (-161, 138, -169, 176, -99, -91, -122, 153, 122),
+    (224, -114, 161, 114, -185, 192, -139, 208, -146, 185, 146),
+    (-123, -154, 169, 154, -225, -177, 225, -115, -162, 130, 162),
+    (232, -193, 177, -186, 193, -147, 186),
+    (-226, 216, -131, 200, -233, -155, -209, 226, -194, 233, 194, -163, -170, 170, -187, -178, 178, -195, -227, 227, -217, 209, 217, -171, -201, 201, -234, 234, -218, 218, -179, -210, 210, -202, -235, -228, 235, 228, -219, 202, -229, -211, -236, -203),
 )
 
 
@@ -364,9 +375,8 @@
             return carry
 
         settle(6)
-        for j0 in range(0, 6, 3):
-            chains.at()
-            lax.fori_loop(j0, j0 + 3, pair, 0)
+        chains.at()
+        lax.fori_loop(0, 6, pair, 0)
         save(layer, 5, attended)
         save(layer, 6, probs)
         chains.at()
@@ -535,7 +545,7 @@
 
 def norm_back(source, upstream, gain_row, gradient, rounded):
     def block(t, sums):
-        rows = pl.ds(pl.multiple_of(t * 64, 64), 64)
+        rows = pl.ds(pl.multiple_of(t * 128, 128), 128)
         inputs = source[rows, :]
         centered = inputs - jnp.mean(inputs, axis=-1, keepdims=True)
         rate = lax.rsqrt(jnp.mean(centered * centered, axis=-1, keepdims=True) + EPSILON)
@@ -554,7 +564,7 @@
         )
 
     zero = jnp.zeros((1, source.shape[1]), F32)
-    return lax.fori_loop(0, source.shape[0] // 64, block, (zero, zero, zero))
+    return lax.fori_loop(0, source.shape[0] // 128, block, (zero, zero, zero))
 
 
 def backward_kernel(*refs):
@@ -622,11 +632,12 @@
     fetch(GRAD, [(first_grad, held[3])])
     fetch(COT, [(cotangent, rounded)])
     fetch(SLOT_A, weights_into(slot_a, 1, "d"))
-    for name in (SLOPE, ACTIVE, MIDDLE, TURNED_MID):
+    for name in (SLOPE, MIDDLE, TURNED_MID):
         fetch_saved(name, 1)
     fetch(SLOT_B, weights_into(slot_b, 1, "u"))
     for name in (ATTENDED, PROJECT, TURNED, STREAM):
         fetch_saved(name, 1)
+    fetch_saved(ACTIVE, 0)
     prob_copy(1, 0).start()
     slots = {("d", 1): (SLOT_A, slot_a), ("u", 1): (SLOT_B, slot_b), ("q", 1): (SLOT_A, slot_a),
              ("d", 0): (SLOT_B, slot_b), ("u", 0): (SLOT_A, slot_a), ("q", 0): (SLOT_B, slot_b)}
@@ -811,7 +822,7 @@
             weight_gradient(first, left, lambda half, cols: active[half, :, cols])
         ready(name)
         ready(SLOPE)
-        place_at()
+        place_at(*([first] if first else []))
 
         def unit(t, carry):
             half = t // 3
@@ -824,32 +835,14 @@
 
         lax.fori_loop(0, 6, unit, 0)
         if layer == 1:
-            ready(ACTIVE)
-            ready(MIDDLE)
-
-            def close(c, carry):
-                cols = pl.ds(pl.multiple_of(c * 384, 128), 384)
-                total = middle[:, cols] + outb[1, 1:2, cols]
-                for half in range(2):
-                    total += mm(active[half], matrix(w_down, half, pl.ds(2 * c, 2)), ((1,), (1,)))
-                dattended[c] = total.astype(BF16)
-                return carry
-
-            lax.fori_loop(0, 2, close, 0)
-            finals = [
-                pltpu.make_async_copy(dattended.at[c], final.at[:, pl.ds(c * 384, 384)], final_sem.at[c])
-                for c in range(2)
-            ]
-            for copy in finals:
-                copy.start()
             fetch(SLOT_A, weights_into(slot_a, 1, "q"))
-            fetch_saved(ACTIVE, 0)
         else:
             fetch(SLOT_B, weights_into(slot_b, 0, "q"))
+            fetch_saved(ACTIVE, 1)
         name, w_up = slots["u", layer]
         ready(name)
         ready(TURNED_MID)
-        place_at(*([first] if first else []))
+        place_at()
         weight_gradient(first + 1, turned_mid, lambda half, cols: slope[half, :, cols])
         place_at(first + 1)
 
@@ -864,25 +857,21 @@
             fetch(SLOT_B, weights_into(slot_b, 0, "d"))
             fetch_saved(SLOPE, 0)
             fetch_saved(TURNED_MID, 0)
-        if layer == 0:
-            ready(MIDDLE)
+        else:
+            fetch(SLOT_A, weights_into(slot_a, 1, "d"))
+        ready(MIDDLE)
         place_at()
         gain_sum, shift_sum, bias_sum = norm_back(middle, upstream, gain[layer, 1:2], gradient, rounded)
         sums[layer, 0:1, 768:1536] = gain_sum
         sums[layer, 1:2, 768:1536] = shift_sum
         sums[layer, 2:3, 0:768] = bias_sum
-        if layer == 1:
-            fetch_saved(MIDDLE, 0)
+        fetch_saved(MIDDLE, 1 - layer)
         name, w_qo = slots["q", layer]
         ready(name)
         ready(ATTENDED)
         place_at()
         turn_rows(rounded, left, k)
         weight_gradient(first + 2, left, lambda half, cols: attended[:, pl.ds(pl.multiple_of(half * 384, 128), 384)])
-
-        if layer == 1:
-            for copy in finals:
-                copy.wait()
 
         def pull_out(half, carry):
             dattended[half] = mm(rounded[...], matrix(w_qo, half, *everything, pl.ds(1152, 384)), ((1,), (0,))).astype(BF16)
@@ -965,8 +954,29 @@
     last = pltpu.make_async_copy(gradient, token_grad, last_sem)
     last.start()
 
+    ready(SLOT_A)
+    ready(ACTIVE)
+    ready(MIDDLE)
+
+    def close(c, carry):
+        cols = pl.ds(pl.multiple_of(c * 384, 128), 384)
+        total = middle[:, cols] + outb[1, 1:2, cols]
+        for half in range(2):
+            total += mm(active[half], matrix(slot_a, half, pl.ds(2 * c, 2)), ((1,), (1,)))
+        dattended[c] = total.astype(BF16)
+        return carry
+
+    chains.at()
+    lax.fori_loop(0, 2, close, 0)
+    finals = [
+        pltpu.make_async_copy(dattended.at[c], final.at[:, pl.ds(c * 384, 384)], final_sem.at[c]) for c in range(2)
+    ]
+    for copy in finals:
+        copy.start()
     chains.at()
     last.wait()
+    for copy in finals:
+        copy.wait()
 
 
 def backward(whole, saved, first_grad, cotangent, lengths, gain, outb):

time: 295 us -> 286 us (0.969)
  Pallas kernels: 294 us -> 285 us
    pallas_call x1, Pallas kernels: 154 us -> 146 us  [backward(): pl.pallas_call(backward_kernel, out_shape=[jax.ShapeDtypeStruct((2, 48, w...]
where the time goes in v2:
time: 286 us
  Pallas kernels  285 us (100%)
    pallas_call x1, Pallas kernels, backward(): pl.pallas_call(backward_kernel, out_shape=[jax.ShapeDtypeStruct((2, 48, w...  146 us
    pallas_call x1, Pallas kernels, forward(): pl.pallas_call(forward_kernel, out_shape=out_shape, in_specs=[any_spec] *...  134 us

profile of v2, /device:TPU:0, one launch (start us, length us, event | category | flops | bytes accessed | tf_op | source)
XLA Modules:
  0.0 285.5 jit_solution(14684666797417199343)
XLA Ops:
  0.6 134.1 %forward.1 = (bf16[2,4,2,2,48,1152]{5,4,3,2,1,0:T(8,128)(2,1)}, bf16[2,4,2,2,48,384]{5,4,3,2,1,0:T(8,128)(2,1)}, bf16[2,4,2,2,48,1536]{5,4,3,2,1,0:T(8,128)(2,1)...) custom-call(bf16[2,3,48,384]{3,2,1,0:T(8,128)(2,1)} %bitcast.7, ...), custom_call_target="tpu_custom_call" | custom-call | tf_op jit(solution)/shard_map/forward/pallas_call | solution.py:505
  134.7 145.7 %backward.1 = (f32[2,48,1152]{2,1,0:T(8,128)}, f32[2,48,384]{2,1,0:T(8,128)}, f32[2,48,1536]{2,1,0:T(8,128)}, f32[2,48,1536]{2,1,0:T(8,128)}, f32[512,768]{1,0:T...) custom-call(bf16[2,4,2,2,48,1152]{5,4,3,2,1,0:T(8,128)(2,1)} %get-tuple-element.57.refs_0_, ...), custom_call_target="tpu_custom_call" | custom-call | tf_op jit(solution)/shard_map/backward/pallas_call | solution.py:1002
  280.5 4.9 %finish.1 = (bf16[512,768]{1,0:T(8,128)(2,1)}, f32[512,768]{1,0:T(8,128)}, f32[2,2,768]{2,1,0:T(2,128)}, f32[2,2,768]{2,1,0:T(2,128)}, f32[2,3,48,384]{3,2,1,0:T...) custom-call(f32[2,48,1152]{2,1,0:T(8,128)} %get-tuple-element.84.ref, ...), custom_call_target="tpu_custom_call" | custom-call | tf_op jit(solution)/shard_map/finish/pallas_call | solution.py:1228

commit v3 on v2

--- a/solution.py
+++ b/solution.py
@@ -70,10 +70,10 @@
 
 
 REDUCE_CHAINS = (
-    (0, 0, 384, "yxz"),
-    (0, 384, 384, "xyz"),
-    (0, 768, 384, "yzx"),
-    (0, 1152, 384, "xzy"),
+    (0, 0, 384, "yzx"),
+    (0, 384, 384, "xzy"),
+    (0, 768, 384, "yxz"),
+    (0, 1152, 384, "xyz"),
     (1, 0, 384, "yxz"),
     (1, 384, 384, "xyz"),
     (1, 768, 384, "yzx"),
@@ -101,32 +101,32 @@
 )
 REDUCE_TABLE = (
     (),
-    (8, 24, 16, 0),
+    (24, 8, 0, 16),
     (),
     (),
     (),
-    (56, 32, -9, 40, -17, 48, 17),
-    (-1, 9, -25, 1, 25),
+    (56, 32, -1, 48, 1, -25, 40),
+    (-9, 9, -17, 17, 25),
+    (-2,),
+    (-33, 72, -57, 33, 57),
+    (-10, -41, 2, -49, 41, 49),
+    (-18, 64, 18, -26, 10, -73),
+    (80, -58, 26, -34, 73, -3, 88, -42, 58, -11, 96),
+    (-65, 104, -50, 34, -74, 50, -19, 74, -81, 65),
+    (-59, -89, 81, 89, -27, 42),
     (),
-    (-18, -33, 72, -57, 18, 57),
-    (-26, -41, 33, -49, 41, 49),
-    (-2, 64, 2, -10, 26, -19),
-    (104, -73, 80, -58, 10, -34, 73, -42, 58, -27, 96),
-    (-65, 88, -50, 34, -3, 42),
-    (-81, 65, -105, 81, -59, 105, -74, 50),
-    (-11, 74),
-    (-35, -89, 136, -97, 128),
-    (-82, 97, 82, -43, -66, 112, 66, -51, 120, -75, -106, 89, 106),
-    (-137, 152, -129, 144, -83, 137),
-    (-98, 168, -67, 129, -107, 98, -113, 160, -90, -121, 113, 121),
+    (-35, -105, 136, -75, -97, 112, -51, 120),
+    (-66, 128, 66, -82, 97, 82, -43, -90, 105, 90),
+    (-137, 168, -113, 144, -67, 137),
+    (-83, -121, 113, -91, -129, 121, 129, -106, 160, 106, -98, 152),
     (),
-    (-138, 90, -145, 184),
-    (-153, 145, -130),
-    (-161, 138, -169, 176, -99, -91, -122, 153, 122),
-    (224, -114, 161, 114, -185, 192, -139, 208, -146, 185, 146),
-    (-123, -154, 169, 154, -225, -177, 225, -115, -162, 130, 162),
-    (232, -193, 177, -186, 193, -147, 186),
-    (-226, 216, -131, 200, -233, -155, -209, 226, -194, 233, 194, -163, -170, 170, -187, -178, 178, -195, -227, 227, -217, 209, 217, -171, -201, 201, -234, 234, -218, 218, -179, -210, 210, -202, -235, -228, 235, 228, -219, 202, -229, -211, -236, -203),
+    (-138, 98, -145, 138, -169, 145),
+    (-122, 169, -114, 176, -130, 114),
+    (-107, 122, -161, 184, -99, -153, 161, -139, 153),
+    (224, -115, -146, 200, 146, -170, 208, 170),
+    (-185, 192, -123, -177, 185, -225, -154, 177, 154, -162, 225, -147, 162),
+    (232, -171),
+    (-201, 130, -209, 201, -186, 209, 186, -233, -226, 233, -155, -193, 226, -131, 193, -163, -178, 178, -187, -202, 202, -210, 216, 210, -234, 234, -227, -179, 227, -194, -235, -203, 235, -217, 217, -211, 194, -218, -228, 218, 228, -236, -229, -195, -219),
 )
 
 

time: 286 us -> 285 us (level)
  no operation moved by 1% of the time
where the time goes in v3:
time: 285 us
  Pallas kernels  284 us (100%)
    pallas_call x1, Pallas kernels, backward(): pl.pallas_call(backward_kernel, out_shape=[jax.ShapeDtypeStruct((2, 48, w...  145 us
    pallas_call x1, Pallas kernels, forward(): pl.pallas_call(forward_kernel, out_shape=out_shape, in_specs=[any_spec] *...  134 us

profile of v3, /device:TPU:0, one launch (start us, length us, event | category | flops | bytes accessed | tf_op | source)
XLA Modules:
  0.0 284.8 jit_solution(15684347877239215889)
XLA Ops:
  0.6 134.1 %forward.1 = (bf16[2,4,2,2,48,1152]{5,4,3,2,1,0:T(8,128)(2,1)}, bf16[2,4,2,2,48,384]{5,4,3,2,1,0:T(8,128)(2,1)}, bf16[2,4,2,2,48,1536]{5,4,3,2,1,0:T(8,128)(2,1)...) custom-call(bf16[2,3,48,384]{3,2,1,0:T(8,128)(2,1)} %bitcast.7, ...), custom_call_target="tpu_custom_call" | custom-call | tf_op jit(solution)/shard_map/forward/pallas_call | solution.py:505
  134.7 145.0 %backward.1 = (f32[2,48,1152]{2,1,0:T(8,128)}, f32[2,48,384]{2,1,0:T(8,128)}, f32[2,48,1536]{2,1,0:T(8,128)}, f32[2,48,1536]{2,1,0:T(8,128)}, f32[512,768]{1,0:T...) custom-call(bf16[2,4,2,2,48,1152]{5,4,3,2,1,0:T(8,128)(2,1)} %get-tuple-element.57.refs_0_, ...), custom_call_target="tpu_custom_call" | custom-call | tf_op jit(solution)/shard_map/backward/pallas_call | solution.py:1002
  279.8 4.9 %finish.1 = (bf16[512,768]{1,0:T(8,128)(2,1)}, f32[512,768]{1,0:T(8,128)}, f32[2,2,768]{2,1,0:T(2,128)}, f32[2,2,768]{2,1,0:T(2,128)}, f32[2,3,48,384]{3,2,1,0:T...) custom-call(f32[2,48,1152]{2,1,0:T(8,128)} %get-tuple-element.84.ref, ...), custom_call_target="tpu_custom_call" | custom-call | tf_op jit(solution)/shard_map/finish/pallas_call | solution.py:1228
